TPU v7x, 32 devices: a whole 2x2x4 slice. The times are simulated.
32 devices in a mesh: seq: 4 (over y, core), ctx: 8 (over z, x).
Axes of the slice: x: 2, y: 2, z: 4, core: 2. Of those that a mesh axis runs over, the one named last changes fastest.
Arguments:
- layer_input: bfloat16 [4, 1024, 1024], P('seq', 'ctx')
- document_ids: int32 [4, 1024], P('seq', 'ctx'), may hold values from 0 to 3, never falling along the last dimension, each value on 1 to 512 neighbouring positions
- expert_routes: int32 [4, 1024, 8], P('seq', 'ctx'), may hold values from 0 to 15, all different within a row; in each aligned block of 128 rows (0 to 127, 128 to 255, ..., all dimensions but the last counted through in order) at most 96 rows name the same one
- rope_factor: float32 [1], replicated, may hold values from 1 to 4
- attention_gain: float32 [1024], P(('seq', 'ctx')), may hold values from 0.25 to 1.75
- feedforward_gain: float32 [1024], P(('seq', 'ctx')), may hold values from 0.25 to 1.75
- query_weight: float32 [1024, 1024], P(('seq', 'ctx')), may hold values from -0.1875 to 0.1875
- key_weight: float32 [1024, 512], P(('seq', 'ctx')), may hold values from -0.1875 to 0.1875
- value_weight: float32 [1024, 512], P(('seq', 'ctx')), may hold values from -0.1875 to 0.1875
- output_weight: float32 [1024, 1024], P(('seq', 'ctx')), may hold values from -1.5 to 1.5
- router_weight: float32 [1024, 16], P(('seq', 'ctx')), may hold values from -0.375 to 0.375
- gate_up: float32 [1024, 16, 1024], P(('seq', 'ctx')), may hold values from -0.1875 to 0.1875
- down_weight: float32 [512, 16, 1024], P(('seq', 'ctx')), may hold values from -0.25 to 0.25
- cotangent: bfloat16 [4, 1024, 1024], P('seq', 'ctx'), may hold values from -6 to 6
Outputs:
- layer_output: bfloat16 [4, 1024, 1024], P('seq', 'ctx')
- input_gradient: bfloat16 [4, 1024, 1024], P('seq', 'ctx')
- attention_gain_gradient: float32 [1024], P(('seq', 'ctx'))
- feedforward_gain_gradient: float32 [1024], P(('seq', 'ctx'))
- query_gradient: float32 [1024, 1024], P(('seq', 'ctx'))
- key_gradient: float32 [1024, 512], P(('seq', 'ctx'))
- value_gradient: float32 [1024, 512], P(('seq', 'ctx'))
- output_gradient: float32 [1024, 1024], P(('seq', 'ctx'))
- router_gradient: float32 [1024, 16], P(('seq', 'ctx'))
- gate_up_gradient: float32 [1024, 16, 1024], P(('seq', 'ctx'))
- down_gradient: float32 [512, 16, 1024], P(('seq', 'ctx'))
Inputs may be any that keep to these rules, and one draw needn't show every extreme that they name: `document_ids`: document ids never fall along a sequence; each of the 4 documents holds 1 to 512 tokens, and one holds exactly 512. `expert_routes`: each token names 8 different experts. Among the 128 tokens of one device (aligned blocks of a sequence) no expert is named by more than 96 tokens, and in some block some expert is named by exactly 96.
All inputs are finite; a program needn't handle non-finite values.
Results may differ from a plain program's by a relative error of at most 0.025.
Values may be sent and summed in bfloat16 or wider, within the bound.
A program may use at most 320 MiB of HBM per device.

v0:
```python
import functools
import math

import jax
import jax.numpy as jnp
from jax import lax
from jax.experimental import pallas as pl
from jax.experimental.pallas import tpu as pltpu
from jax.sharding import PartitionSpec as P

HEADS = 16
KV_HEADS = 8
HEAD_DIM = 64
GROUP = HEADS // KV_HEADS
HEAD_COLS = (GROUP + 2) * HEAD_DIM

NORM_EPS = 1e-06
ROPE_BASE = 10000.0
NEG_BIG = -1e30
LOW = jnp.bfloat16
WIDE = jnp.float32
MESH = pl.DeviceIdType.MESH


def ring_place(index, size):
    half = index // 2
    return half + (index % 2) * (size - 1 - 2 * half)


def ring_member(place, size):
    place = (place + 2 * size) % size
    far = place // (size // 2)
    return 2 * place + far * (2 * size - 1 - 4 * place)


def slot_of(distance, size):
    if distance == 0:
        return 0
    if abs(distance) == size // 2:
        return 1
    return 2 * abs(distance) + (distance > 0)


def core_mate(index):
    return index + 1 - 2 * (index % 2)


def row_mate(index):
    return (index + 2) % 4


def push(src, dst, send, recv, **where):
    return pltpu.make_async_remote_copy(
        src_ref=src, dst_ref=dst, send_sem=send, recv_sem=recv, device_id=where, device_id_type=MESH
    )


def greet(peers):
    barrier = pltpu.get_barrier_semaphore()
    for where in peers:
        pl.semaphore_signal(barrier, inc=1, device_id=where, device_id_type=MESH)
    pl.semaphore_wait(barrier, len(peers))


def ring_peers(size):
    place = ring_place(lax.axis_index("ctx"), size)
    return ring_member(place + 1, size), ring_member(place - 1, size)


class RingGather:
    def __init__(self, size, source, target, send, recv, relative=False):
        self.size, self.source, self.target, self.send, self.recv = size, source, target, send, recv
        self.relative = relative
        self.place = ring_place(lax.axis_index("ctx"), size)
        self.right, self.left = ring_peers(size)
        self.steps = size // 2

    def _copy(self, way, step, arriving):
        sign = 2 * way - 1
        rows = self.source.shape[0]
        part = pl.ds(way * (rows // 2), rows // 2) if step == self.steps - 1 else pl.ds(0, rows)
        if self.relative:
            here, there = slot_of(sign * step, self.size), slot_of(sign * (step + 1), self.size)
        else:
            here = there = ring_member(self.place + sign * (step + arriving), self.size)
        dst = self.target.at[there, part]
        src = self.target.at[here, part] if step else self.source.at[part]
        where = self.left if way else self.right
        return push(dst if arriving else src, dst, self.send.at[way, step], self.recv.at[way, step], ctx=where)

    def start(self, step):
        for way in range(2):
            if step:
                self._copy(way, step - 1, 1).wait_recv()
            self._copy(way, step, 0).start()

    def land(self):
        for way in range(2):
            self._copy(way, self.steps - 1, 1).wait_recv()

    def drain(self):
        for way in range(2):
            for step in range(self.steps):
                self._copy(way, step, 0).wait_send()

    def finish(self):
        self.land()
        self.drain()


def row_step(rows):
    return rows if rows < 16 else 16


def sum_into(target, parts):
    rows = target.shape[-2]
    step = row_step(rows)

    def add_at(lead):
        def body(r, _):
            at = lead + (pl.ds(pl.multiple_of(r * step, step), step),)
            total = parts[0][at].astype(WIDE)
            for part in parts[1:]:
                total = total + part[at].astype(WIDE)
            target[at] = total.astype(target.dtype)
            return 0

        lax.fori_loop(0, rows // step, body, 0)

    for lead in [()] if target.ndim == 2 else [(u,) for u in range(target.shape[0])]:
        add_at(lead)


def dot_nn(a, b):
    return lax.dot_general(a, b, (((1,), (0,)), ((), ())), preferred_element_type=WIDE)


def dot_nt(a, b):
    return lax.dot_general(a, b, (((1,), (1,)), ((), ())), preferred_element_type=WIDE)


def dot_tn(a, b):
    return lax.dot_general(a, b, (((0,), (0,)), ((), ())), preferred_element_type=WIDE)


class RingReduce:
    def __init__(self, size, held, send, recv):
        self.size, self.held, self.send, self.recv = size, held, send, recv
        self.place = ring_place(lax.axis_index("ctx"), size)
        self.right, self.left = ring_peers(size)
        self.steps = size // 2
        self.rows = held.shape[2]

    def owner(self, way, step):
        ahead = self.steps - step
        return ring_member(self.place + ahead if way == 0 else self.place - ahead, self.size)

    def _copy(self, way, step, source):
        half = self.rows // 2
        part = pl.ds(0, self.rows) if step else pl.ds(half * way, half)
        where = self.right if way == 0 else self.left
        return push(
            source, self.held.at[way, step, part], self.send.at[way, step], self.recv.at[way, step], ctx=where
        )

    def start(self, step, own):
        for way in range(2):
            half = self.rows // 2
            near = pl.ds(0, half) if way == 0 else pl.ds(half, half)
            far = pl.ds(half, half) if way == 0 else pl.ds(0, half)
            source = own[way].at[near]
            if step:
                self._copy(way, step - 1, source).wait_recv()
                source = self.held.at[way, step - 1]
                if step == 1:
                    sum_into(source.at[near], [own[way].at[near], source.at[near]])
                    sum_into(source.at[far], [own[way].at[far]])
                else:
                    sum_into(source, [own[way], source])
            self._copy(way, step, source).start()

    def finish(self, target, own, first):
        last, half = self.steps - 1, self.rows // 2
        for way in range(2):
            self._copy(way, last, self.held.at[way, last]).wait_recv()
        sum_into(target, [own, self.held.at[0, last], self.held.at[1, last]])
        for way in range(2):
            for step in range(self.steps):
                source = self.held.at[way, step - 1] if step else first.at[pl.ds(half * way, half)]
                self._copy(way, step, source).wait_send()


def expert_kernel(
    size, split,
    expert_input, combine_rows, upstream, gu_hbm, down_hbm,
    mix, back_sum, gate_home, gu_grads, down_grads,
    tokens_all, combine_all, gu_weight, down_weight, combine_cols, gate_up, hidden, both_grad, out_acc, out_own,
    back_own, gate_send, held_out, held_back,
    send_b, recv_b, send_c, recv_c, send_y, recv_y, send_d, recv_d, send_g, recv_g, own_sem,
):
    me = lax.axis_index("ctx")
    place = ring_place(me, size)
    per_unit, width, ff2 = gu_weight.shape
    ff = ff2 // 2
    tokens = expert_input.shape[0]
    group = 2 * tokens
    groups = size // 2
    first_expert = me // split * per_unit
    greet([{"ctx": (me + k) % size} for k in range(1, size)])

    loads = [
        pltpu.make_async_copy(expert_input, tokens_all.at[0], own_sem.at[0]),
        pltpu.make_async_copy(combine_rows, combine_all.at[0], own_sem.at[1]),
        pltpu.make_async_copy(gu_hbm, gu_weight, own_sem.at[2]),
        pltpu.make_async_copy(down_hbm, down_weight, own_sem.at[3]),
    ]
    rings = [
        RingGather(size, combine_rows, combine_all, send_c, recv_c, True),
        RingGather(size, expert_input, tokens_all, send_b, recv_b, True),
    ]
    for ring in rings:
        ring.start(0)
    for load in loads:
        load.start()
    for load in loads:
        load.wait()
    lanes = lax.broadcasted_iota(jnp.int32, (group, 128), 1)

    def forward(turn, _):
        for step in range(1, groups):
            @pl.when(turn == step - 1)
            def _():
                for ring in rings:
                    ring.start(step)

        @pl.when(turn == groups - 1)
        def _():
            for ring in rings:
                ring.land()

        g = (turn + 1) % groups
        pair = pl.ds(2 * g, 2)
        rows = pl.ds(pl.multiple_of(g * group, group), group)
        token = tokens_all[pair].reshape(group, width)
        up_wide = upstream[pair].reshape(group, width).astype(WIDE)
        weights = jnp.concatenate([combine_all[2 * g].T, combine_all[2 * g + 1].T], axis=0)
        names = lax.broadcasted_iota(jnp.int32, weights.shape, 1)
        out_acc[...] = jnp.zeros_like(out_acc)

        def one(e, gates):
            weight = jnp.sum(jnp.where(names == first_expert + e, weights, 0.0), axis=1, keepdims=True)
            combine_cols[e, rows] = jnp.broadcast_to(weight, (group, 128))
            both = dot_nn(token, gu_weight[e])
            gate_up[e, rows] = both.astype(gate_up.dtype)
            gate, up = both[:, :ff], both[:, ff:]
            hid = (gate / (1.0 + jnp.exp(-gate)) * up).astype(LOW)
            hidden[e, rows] = hid
            produced = dot_nn(hid, down_weight[e])
            out_acc[...] += weight * produced
            dg = jnp.sum(up_wide * produced, axis=1, keepdims=True)
            return jnp.where(lanes == e, dg, gates)

        gates = lax.fori_loop(0, per_unit, one, jnp.zeros((group, 128), WIDE)).T
        gate_send[2 * g] = gates[:8, :tokens]
        gate_send[2 * g + 1] = gates[:8, tokens:]
        out_own[pair] = out_acc[...].astype(LOW).reshape(2, tokens, width)
        return 0

    lax.fori_loop(0, groups, forward, 0)

    def gate_copy(distance):
        there = ring_member(place + distance, size)
        k = distance % size
        return push(gate_send.at[slot_of(distance, size)], gate_home.at[me], send_g.at[k], recv_g.at[k], ctx=there)

    distances = [d for d in range(1 - groups, groups + 1) if d]
    for distance in distances:
        gate_copy(distance).start()
    gate_home[me] = gate_send[0]

    ring_out = RingReduce(size, held_out, send_y, recv_y)
    ring_back = RingReduce(size, held_back, send_d, recv_d)

    def backward(turn, _):
        for step in range(groups):
            @pl.when(turn == step)
            def _():
                ring_out.start(
                    step, [out_own.at[slot_of(groups - step, size)], out_own.at[slot_of(step - groups, size)]]
                )

        g = (groups - turn) % groups
        pair = pl.ds(2 * g, 2)
        rows = pl.ds(pl.multiple_of(g * group, group), group)
        up_wide = upstream[pair].reshape(group, width).astype(WIDE)
        out_acc[...] = jnp.zeros_like(out_acc)

        def one(e, _):
            weight = combine_cols[e, rows][:, 0:1]
            grad = (weight * up_wide).astype(LOW)
            hid_grad = dot_nt(grad, down_weight[e])
            gate = gate_up[e, rows, pl.ds(0, ff)].astype(WIDE)
            up = gate_up[e, rows, pl.ds(ff, ff)].astype(WIDE)
            sigmoid = 1.0 / (1.0 + jnp.exp(-gate))
            gate_part = (hid_grad * up * sigmoid * (1.0 + gate * (1.0 - sigmoid))).astype(LOW)
            up_part = (hid_grad * (gate * sigmoid)).astype(LOW)
            both_grad[e, rows, pl.ds(0, ff)] = gate_part
            both_grad[e, rows, pl.ds(ff, ff)] = up_part
            out_acc[...] += dot_nt(both_grad[e, rows], gu_weight[e])
            return 0

        lax.fori_loop(0, per_unit, one, 0)
        near = 2 * ((g + groups - 1) // groups)
        back_own[pl.ds(near, 2)] = out_acc[...].astype(LOW).reshape(2, tokens, width)
        for step in range(groups):
            @pl.when(turn == step)
            def _():
                ring_back.start(step, [back_own.at[1]] * 2 if step == 0 else [back_own.at[3], back_own.at[2]])
        return 0

    lax.fori_loop(0, groups, backward, 0)

    tile = 256
    length = size * tokens

    def gu_tile(j, _):
        turned = tokens_all[:, :, pl.ds(pl.multiple_of(j * tile, tile), tile)].reshape(length, tile)
        turned = turned.astype(WIDE).T.astype(LOW)
        depth = gu_grads.shape[2]
        count = tile // depth

        def one(e, _):
            part = dot_nn(turned, both_grad[e]).reshape(count, depth, ff2)
            gu_grads[e, pl.ds(j * count, count)] = part.astype(LOW)
            return 0

        return lax.fori_loop(0, per_unit, one, 0)

    lax.fori_loop(0, width // tile, gu_tile, 0)

    def down_tile(index, _):
        e, j = index // (ff // tile), index % (ff // tile)
        turned = hidden[e, :, pl.ds(pl.multiple_of(j * tile, tile), tile)].astype(WIDE).T.astype(LOW)
        depth = down_grads.shape[2]
        count = tile // depth
        for half in range(2):
            cols = pl.ds(half * (width // 2), width // 2)
            grad = upstream[:, :, cols].reshape(length, width // 2).astype(WIDE) * combine_cols[e][:, 0:1]
            part = dot_nn(turned, grad.astype(LOW)).reshape(count, depth, width // 2)
            down_grads[e, pl.ds(j * count, count), :, cols] = part.astype(LOW)
        return 0

    lax.fori_loop(0, per_unit * (ff // tile), down_tile, 0)

    ring_back.finish(back_sum, back_own.at[0], back_own.at[1])
    ring_out.finish(mix, out_own.at[0], out_own.at[1])
    for ring in rings:
        ring.drain()
    for distance in distances:
        here = ring_member(place - distance, size)
        k = distance % size
        push(gate_send.at[0], gate_home.at[here], send_g.at[k], recv_g.at[k], ctx=here).wait_recv()
        gate_copy(distance).wait_send()


def run_experts(expert_input, combine_rows, upstream, gu_full, down_full, size, split, owners, down_rows, collective):
    tokens, width = expert_input.shape
    per_unit, _, ff2 = gu_full.shape
    ff = ff2 // 2
    length = size * tokens
    dma = pltpu.SemaphoreType.DMA
    vmem = pl.BlockSpec(memory_space=pltpu.VMEM)
    anywhere = pl.BlockSpec(memory_space=pl.ANY)
    steps = (2, size // 2)
    return pl.pallas_call(
        functools.partial(expert_kernel, size, split),
        out_shape=[
            jax.ShapeDtypeStruct((tokens, width), WIDE),
            jax.ShapeDtypeStruct((tokens, width), WIDE),
            jax.ShapeDtypeStruct((size, 8, tokens), WIDE),
            jax.ShapeDtypeStruct((per_unit, owners, width // owners, ff2), LOW),
            jax.ShapeDtypeStruct((per_unit, ff // down_rows, down_rows, width), LOW),
        ],
        in_specs=[vmem, vmem, vmem, anywhere, anywhere],
        out_specs=[vmem] * 5,
        scratch_shapes=[
            pltpu.VMEM((size, tokens, width), LOW),
            pltpu.VMEM((size,) + combine_rows.shape, WIDE),
            pltpu.VMEM(gu_full.shape, LOW),
            pltpu.VMEM(down_full.shape, LOW),
            pltpu.VMEM((per_unit, length, 128), WIDE),
            pltpu.VMEM((per_unit, length, ff2), WIDE if length <= 2048 else LOW),
            pltpu.VMEM((per_unit, length, ff), LOW),
            pltpu.VMEM((per_unit, length, ff2), LOW),
            pltpu.VMEM((2 * tokens, width), WIDE),
            pltpu.VMEM((size, tokens, width), LOW),
            pltpu.VMEM((4, tokens, width), LOW),
            pltpu.VMEM((size, 8, tokens), WIDE),
            pltpu.VMEM((2, size // 2, tokens, width), LOW),
            pltpu.VMEM((2, size // 2, tokens, width), LOW),
            dma(steps), dma(steps), dma(steps), dma(steps), dma(steps), dma(steps), dma(steps), dma(steps),
            dma((size,)), dma((size,)), dma((4,)),
        ],
        compiler_params=pltpu.CompilerParams(
            collective_id=collective, has_side_effects=True, vmem_limit_bytes=63 << 20
        ),
        name="run_experts",
    )(expert_input, combine_rows, upstream, gu_full, down_full)


class Spread:
    def __init__(self, size, source, slab, sems):
        self.size, self.source, self.slab = size, source, slab
        self.send_a, self.recv_a, self.send_b, self.recv_b, self.own = sems
        self.me, self.seq = lax.axis_index("ctx"), lax.axis_index("seq")

    def _from(self, k):
        return (self.me + self.size - k) % self.size

    def local(self):
        return pltpu.make_async_copy(self.source(self.me), self.slab(self.seq * self.size + self.me), self.own)

    def outward(self, k):
        there = (self.me + k) % self.size
        slab = self.slab(self.seq * self.size + self.me)
        return push(self.source(there), slab, self.send_a.at[k], self.recv_a.at[k], ctx=there)

    def inward(self, k):
        here = self._from(k)
        slab = self.slab(self.seq * self.size + here)
        return push(self.source(here), slab, self.send_a.at[k], self.recv_a.at[k], ctx=here)

    def sideways(self, which, k):
        owner = row_mate(self.seq) if which == 2 else self.seq
        slab = self.slab(owner * self.size + self._from(k))
        mate = row_mate(self.seq) if which == 1 else core_mate(self.seq)
        return push(slab, slab, self.send_b.at[which, k], self.recv_b.at[which, k], seq=mate)

    def landing(self, which, k):
        owner = (core_mate(self.seq), row_mate(self.seq), core_mate(row_mate(self.seq)))[which]
        slab = self.slab(owner * self.size + self._from(k))
        return push(slab, slab, self.send_b.at[which, k], self.recv_b.at[which, k], seq=core_mate(self.seq))

    def start(self):
        for k in range(1, self.size):
            self.outward(k).start()

    def step(self, k):
        if k == 0:
            self.local().wait()
        else:
            self.inward(k).wait_recv()
        self.sideways(1, k).start()
        self.sideways(0, k).start()
        if k:
            self.pass_on(k - 1)

    def pass_on(self, k):
        self.landing(1, k).wait_recv()
        self.sideways(2, k).start()

    def land(self):
        for k in range(self.size):
            self.landing(0, k).wait_recv()
            self.landing(2, k).wait_recv()

    def drain(self):
        for k in range(self.size):
            for which in range(3):
                self.sideways(which, k).wait_send()
            if k:
                self.outward(k).wait_send()

    @staticmethod
    def scratch(size):
        dma = pltpu.SemaphoreType.DMA
        return [dma((size,)), dma((size,)), dma((3, size)), dma((3, size)), dma]


def front_kernel(
    size, split, tile,
    tokens_in, upstream, docs_in, cos_turned, sin_turned, pack, gu_pack, down_pack, out_rows,
    inputs_all, upstream_all, mixed, query_pair, key_value, out_pair, log_total, docs_row, docs_col, places_row,
    cosine, sine, row_scale, head_weight, small, gu_full, down_full, out_full,
    docs_all, pack_all, key_pad, value_turned, head_out,
    send_t, recv_t, send_u, recv_u, send_n, recv_n, send_x, recv_x, own, *scratch,
):
    me, seq = lax.axis_index("ctx"), lax.axis_index("seq")
    lane, row, number = me % split, me // split, size // split
    tokens, width = tokens_in.shape
    steps = size // 2
    place = ring_place(me, size)
    greet(
        [{"ctx": (me + k) % size} for k in range(1, size)]
        + [{"seq": core_mate(seq)}, {"seq": row_mate(seq)}]
    )
    heads = Spread(size, lambda c: pack.at[c], lambda owner: pack_all.at[owner], scratch[0:5])
    bulk = [
        Spread(size, lambda c: gu_pack.at[c], lambda owner: gu_full.at[:, owner], scratch[5:10]),
        Spread(size, lambda c: down_pack.at[c], lambda owner: down_full.at[:, owner], scratch[10:15]),
        Spread(size, lambda c: out_rows, lambda owner: out_full.at[owner], scratch[15:20]),
    ]
    ring = RingGather(size, tokens_in, inputs_all, send_t, recv_t)
    ring_up = RingGather(size, upstream, upstream_all, send_u, recv_u, True)

    def note(k):
        return push(docs_in, docs_all.at[me], send_n.at[k], recv_n.at[k], ctx=(me + k) % size)

    def noted(k):
        here = (me + size - k) % size
        return push(docs_in, docs_all.at[here], send_n.at[k], recv_n.at[k], ctx=here)

    heads.start()
    for k in range(1, size):
        note(k).start()
    ring.start(0)
    heads.local().start()
    local = [
        pltpu.make_async_copy(tokens_in, inputs_all.at[me], own.at[0]),
        pltpu.make_async_copy(upstream, upstream_all.at[0], own.at[1]),
    ]
    for copy in local:
        copy.start()
    for part in bulk:
        part.local().start()
    docs_all[me] = docs_in[...]

    def tables(i, _):
        rows = pl.ds(pl.multiple_of(i * tile, tile), tile)
        cos, sin = cos_turned[:, rows], sin_turned[:, rows]
        cosine[rows] = jnp.concatenate([cos] * 4, axis=0).T
        sine[rows] = jnp.concatenate([-sin, sin] * 2, axis=0).T
        return 0

    lax.fori_loop(0, size * tokens // tile, tables, 0)
    for k in range(size):
        heads.step(k)
    heads.pass_on(size - 1)
    for part in bulk:
        part.step(0)
    ring.start(1)
    for k in range(1, size):
        noted(k).wait_recv()
    log_total[...] = jnp.zeros_like(log_total)

    def documents(c, _):
        rows = pl.ds(pl.multiple_of(c * tokens, tokens), tokens)
        docs_col[rows] = docs_all[c].astype(WIDE).T[:, 0:1].astype(jnp.int32)
        return 0

    lax.fori_loop(0, size, documents, 0)

    def my_documents(b, _):
        rows = pl.ds(pl.multiple_of(b * tokens, tokens), tokens)
        docs_row[:, rows] = docs_all[b * split + lane]
        first = (b * split + lane) * tokens
        places_row[:, rows] = lax.broadcasted_iota(jnp.int32, (8, tokens), 1) + first
        return 0

    lax.fori_loop(0, number, my_documents, 0)
    heads.land()
    whole = pack_all[...].astype(WIDE).reshape(width, pack_all.shape[2])
    head_weight[...] = whole[:, :HEAD_COLS].astype(LOW)
    small[...] = whole[:, HEAD_COLS:].T[: small.shape[0]]
    gain_row = small.shape[0] - 8
    for copy in local:
        copy.wait()

    half = lax.broadcasted_iota(jnp.int32, (tokens, 2 * HEAD_DIM), 1) < HEAD_DIM

    def project(spot):
        owner = ring_member(spot, size)
        rows = pl.ds(pl.multiple_of(owner * tokens, tokens), tokens)
        values = inputs_all[owner].astype(WIDE)
        scale_one = lax.rsqrt(jnp.mean(values * values, axis=-1, keepdims=True) + NORM_EPS)
        row_scale[rows] = scale_one
        attend = (values * scale_one * small[gain_row : gain_row + 1]).astype(LOW)
        pre = dot_nn(attend, head_weight[...])
        cos, sin = cosine[rows], sine[rows]
        query, pair = pre[:, : 2 * HEAD_DIM], pre[:, 2 * HEAD_DIM :]
        query = query * cos + swap_halves(query) * sin
        pair = pair * jnp.where(half, cos, 1.0) + swap_halves(pair) * jnp.where(half, sin, 0.0)
        key_value[rows] = pair.astype(LOW)
        key_pad[0, rows] = jnp.where(half, pair, 0.0).astype(LOW)
        key_pad[1, rows] = jnp.where(half, 0.0, pltpu.roll(pair, HEAD_DIM, 1)).astype(LOW)
        value_turned[:, rows] = pair.T[HEAD_DIM:].astype(LOW)

        @pl.when(owner % split == lane)
        def _():
            query_pair[pl.ds(pl.multiple_of(owner // split * tokens, tokens), tokens)] = query.astype(LOW)

    project(place)

    def visit(turn, _):
        for step in range(1, steps):
            @pl.when(turn == step)
            def _():
                if step > 1:
                    ring.start(step)
                if step == steps - 1:
                    ring_up.start(0)
                    for part in bulk:
                        part.start()

        def side(way, _):
            project(place + (2 * way - 1) * turn)
            return 0

        return lax.fori_loop(0, 2, side, 0)

    lax.fori_loop(1, steps, visit, 0)
    ring.land()
    project(place + steps)

    todo = []
    for k in range(1, size):
        todo += [functools.partial(part.step, k) for part in bulk]
        if k % 2 == 0 and k // 2 < steps:
            todo.append(functools.partial(ring_up.start, k // 2))

    def pump(count):
        for _ in range(min(count, len(todo))):
            todo.pop(0)()

    scale = HEAD_DIM**-0.5
    for i in range(number * tokens // tile):
        rows = pl.ds(i * tile, tile)
        query = query_pair[rows]
        query_doc, query_place = docs_row[0:1, rows], places_row[0:1, rows]

        def pairs(j, carry):
            keys = pl.ds(pl.multiple_of(j * tile, tile), tile)
            spot = lax.broadcasted_iota(jnp.int32, (tile, tile), 0) + j * tile
            allowed = (spot <= query_place) & (docs_col[keys] == query_doc)
            found = []
            for h in range(GROUP):
                peak, total, gathered = carry[3 * h : 3 * h + 3]
                score = jnp.where(allowed, dot_nt(key_pad[h, keys], query) * scale, NEG_BIG)
                higher = jnp.maximum(peak, jnp.max(score, axis=0, keepdims=True))
                keep = jnp.exp(peak - higher)
                prob = jnp.exp(score - higher)
                total = total * keep + jnp.sum(prob, axis=0, keepdims=True)
                gathered = gathered * keep + dot_nn(value_turned[:, keys], prob.astype(LOW))
                found += [higher, total, gathered]
            return tuple(found)

        empty = (
            jnp.full((1, tile), NEG_BIG, WIDE), jnp.zeros((1, tile), WIDE), jnp.zeros((HEAD_DIM, tile), WIDE)
        )
        found = lax.fori_loop(0, min(size * tokens // tile, (i + 1) * split), pairs, empty * GROUP)
        for h in range(GROUP):
            log_total[h : h + 1, rows] = found[3 * h] + jnp.log(found[3 * h + 1])
        result = jnp.concatenate([found[3 * h + 2] / found[3 * h + 1] for h in range(GROUP)], axis=0).T
        out_pair[rows] = result
        blocks = tile // tokens
        head_out[pl.ds(i * blocks, blocks)] = result.astype(LOW).reshape(blocks, tokens, 2 * HEAD_DIM)
        pump(3)

    def seat(index):
        return mixed.at[:, pl.ds(pl.multiple_of(index * 2 * HEAD_DIM, 2 * HEAD_DIM), 2 * HEAD_DIM)]

    swaps = []
    for k in range(1, number):
        there = (row + k) % number
        swaps.append(push(head_out.at[there], seat(row), send_x.at[k], recv_x.at[k], ctx=there * split + lane))
        swaps[-1].start()
    mine = pltpu.make_async_copy(head_out.at[row], seat(row), own.at[2])
    mine.start()
    pump(len(todo))
    for part in bulk:
        part.pass_on(size - 1)
    ring_up.land()
    for k in range(1, number):
        here = (row + number - k) % number
        push(head_out.at[here], seat(here), send_x.at[k], recv_x.at[k], ctx=here * split + lane).wait_recv()
    mine.wait()
    for part in bulk:
        part.land()
    for copy in swaps:
        copy.wait_send()
    for k in range(1, size):
        note(k).wait_send()
    ring.drain()
    ring_up.drain()
    for part in [heads] + bulk:
        part.drain()


def run_front(tokens_in, upstream, docs, cos_turned, sin_turned, pack, gu_pack, down_pack, out_rows, split, owners, small_rows,
              collective):
    size = pack.shape[0]
    tokens, width = tokens_in.shape
    length, mine = size * tokens, size * tokens // split
    tile = 2 * tokens
    dma = pltpu.SemaphoreType.DMA
    vmem = pl.BlockSpec(memory_space=pltpu.VMEM)
    anywhere = pl.BlockSpec(memory_space=pl.ANY)
    pair = 2 * HEAD_DIM
    per_unit = gu_pack.shape[1]
    shape = jax.ShapeDtypeStruct
    return pl.pallas_call(
        functools.partial(front_kernel, size, split, tile),
        out_shape=[
            shape((size, tokens, width), LOW), shape((size, tokens, width), LOW),
            shape((tokens, HEADS * HEAD_DIM), LOW), shape((mine, pair), LOW), shape((length, pair), LOW),
            shape((mine, pair), WIDE), shape((8, mine), WIDE), shape((8, mine), jnp.int32),
            shape((length, 1), jnp.int32), shape((8, mine), jnp.int32),
            shape((length, pair), WIDE), shape((length, pair), WIDE), shape((length, 1), WIDE),
            shape((width, HEAD_COLS), LOW), shape((small_rows, width), WIDE),
            shape((per_unit, owners) + gu_pack.shape[2:], LOW),
            shape((per_unit, owners) + down_pack.shape[2:], LOW),
            shape((owners,) + out_rows.shape, LOW),
        ],
        in_specs=[vmem] * 9,
        out_specs=[vmem, anywhere] + [vmem] * 13 + [anywhere] * 3,
        scratch_shapes=[
            pltpu.VMEM((size, 8, tokens), jnp.int32),
            pltpu.VMEM((owners,) + pack.shape[1:], LOW),
            pltpu.VMEM((GROUP, length, pair), LOW),
            pltpu.VMEM((HEAD_DIM, length), LOW),
            pltpu.VMEM((size // split, tokens, pair), LOW),
            dma((2, size // 2)), dma((2, size // 2)), dma((2, size // 2)), dma((2, size // 2)),
            dma((size,)), dma((size,)), dma((size // split,)), dma((size // split,)), dma((3,)),
        ] + Spread.scratch(size) * 4,
        compiler_params=pltpu.CompilerParams(
            collective_id=collective, has_side_effects=True, vmem_limit_bytes=60 << 20
        ),
        name="run_front",
    )(tokens_in, upstream, docs, cos_turned, sin_turned, pack, gu_pack, down_pack, out_rows)


class Homing:
    def __init__(self, size, grads, out, bufs, sems):
        self.size, self.grads, self.out = size, grads, out
        self.near, self.from_core, self.from_row, self.to_row, self.to_home = bufs
        self.load, self.send_a, self.recv_a, self.send_b, self.recv_b, self.send_c, self.recv_c = sems
        self.me, self.seq = lax.axis_index("ctx"), lax.axis_index("seq")

    def _block(self, s0, k):
        index = s0 * self.size + (self.me + k) % self.size
        return self.grads.at[:, index] if self.grads.ndim == 4 else self.grads.at[index]

    def _row(self, which):
        return row_mate(self.seq) if which == 0 else self.seq

    def fetch(self, which, k):
        return pltpu.make_async_copy(self._block(self._row(which), k), self.near.at[which, k], self.load.at[which, k])

    def to_core(self, which, k):
        return push(
            self._block(core_mate(self._row(which)), k), self.from_core.at[which, k],
            self.send_a.at[which, k], self.recv_a.at[which, k], seq=core_mate(self.seq),
        )

    def across(self, k):
        return push(
            self.to_row.at[k], self.from_row.at[k], self.send_b.at[k], self.recv_b.at[k], seq=row_mate(self.seq)
        )

    def homeward(self, k):
        there = (self.me + k) % self.size
        return push(self.to_home.at[k], self.out.at[self.me], self.send_c.at[k], self.recv_c.at[k], ctx=there)

    def arriving(self, k):
        here = (self.me + self.size - k) % self.size
        return push(self.to_home.at[k], self.out.at[here], self.send_c.at[k], self.recv_c.at[k], ctx=here)

    def start(self):
        def body(k, _):
            for which in range(2):
                self.to_core(which, k).start()
                self.fetch(which, k).start()
            return 0

        lax.fori_loop(0, self.size, body, 0)

    def first(self, k):
        self.fetch(0, k).wait()
        self.to_core(0, k).wait_recv()
        sum_into(self.to_row.at[k], [self.near.at[0, k], self.from_core.at[0, k]])
        self.across(k).start()

    def second(self, k, home=False):
        self.fetch(1, k).wait()
        self.to_core(1, k).wait_recv()
        self.across(k).wait_recv()
        target = self.out.at[self.me] if home else self.to_home.at[k]
        sum_into(target, [self.near.at[1, k], self.from_core.at[1, k], self.from_row.at[k]])
        if not home:
            self.homeward(k).start()

    def close(self):
        def body(k, _):
            self.arriving(k).wait_recv()
            self.homeward(k).wait_send()
            return 0

        lax.fori_loop(1, self.size, body, 0)

        def drain(k, _):
            self.to_core(0, k).wait_send()
            self.to_core(1, k).wait_send()
            self.across(k).wait_send()
            return 0

        lax.fori_loop(0, self.size, drain, 0)

    @staticmethod
    def scratch(size, block):
        slab = (size,) + block
        dma = pltpu.SemaphoreType.DMA
        return [
            pltpu.VMEM((2,) + slab, LOW), pltpu.VMEM((2,) + slab, LOW), pltpu.VMEM(slab, LOW),
            pltpu.VMEM(slab, LOW), pltpu.VMEM(slab, LOW),
            dma((2, size)), dma((2, size)), dma((2, size)), dma((size,)), dma((size,)), dma((size,)), dma((size,)),
        ]


class SmallSum:
    def __init__(self, size, small, out, from_seq, total, from_ctx, sems):
        self.size, self.small, self.out = size, small, out
        self.from_seq, self.total, self.from_ctx = from_seq, total, from_ctx
        self.send_a, self.recv_a, self.send_b, self.recv_b = sems
        self.me, self.seq = lax.axis_index("ctx"), lax.axis_index("seq")

    def _swap(self, k):
        there = (self.seq + k) % 4
        return push(self.small.at[there], self.from_seq.at[k], self.send_a.at[k], self.recv_a.at[k], seq=there)

    def _tell(self, k):
        there = (self.me + k) % self.size
        return push(self.total, self.from_ctx.at[self.me], self.send_b.at[k], self.recv_b.at[k], ctx=there)

    def _hear(self, k):
        here = (self.me + self.size - k) % self.size
        return push(self.total, self.from_ctx.at[here], self.send_b.at[k], self.recv_b.at[k], ctx=here)

    def start(self):
        for k in range(1, 4):
            self._swap(k).start()

    def middle(self):
        for k in range(1, 4):
            self._swap(k).wait_recv()
        self.total[...] = self.small[self.seq] + self.from_seq[1] + self.from_seq[2] + self.from_seq[3]
        for k in range(1, self.size):
            self._tell(k).start()

    def finish(self):
        total = self.total[...]
        for k in range(1, self.size):
            self._hear(k).wait_recv()
            total = total + self.from_ctx[(self.me + self.size - k) % self.size]
        self.out[...] = total
        for k in range(1, 4):
            self._swap(k).wait_send()
        for k in range(1, self.size):
            self._tell(k).wait_send()

    @staticmethod
    def scratch(size, rows, lanes):
        dma = pltpu.SemaphoreType.DMA
        part = (rows, lanes // 4)
        return [
            pltpu.VMEM((4,) + part, WIDE), pltpu.VMEM(part, WIDE), pltpu.VMEM((size,) + part, WIDE),
            dma((4,)), dma((4,)), dma((size,)), dma((size,)),
        ]


def back_kernel(
    size, split, tile,
    mixed_grad, gu_grads, down_grads, out_grads, small, query_pair, key_value, out_pair, log_total,
    docs_row, docs_col, places_row, cosine, sine, gain, inputs_all, row_scale, head_weight,
    attend_sum, gu_home, down_home, out_home, head_home, small_home,
    head_grad, key_pad, value_pad, key_acc, value_acc, query_acc, heads_grad, heads_turned, head_part, small_full,
    attend_own, held, send_r, recv_r, send_x, recv_x, own_x, *scratch,
):
    me, seq = lax.axis_index("ctx"), lax.axis_index("seq")
    lane, row, number = me % split, me // split, size // split
    tokens = mixed_grad.shape[1]
    length, width = inputs_all.shape
    greet(
        [{"ctx": (me + k) % size} for k in range(1, size)]
        + [{"seq": (seq + k) % 4} for k in range(1, 4)]
    )

    def homing(i, grads, out):
        part = scratch[12 * i : 12 * i + 12]
        return Homing(size, grads, out, part[:5], part[5:])

    early = [homing(0, gu_grads, gu_home), homing(1, down_grads, down_home), homing(2, out_grads, out_home)]
    late = homing(3, head_part, head_home)
    tail = scratch[48:]
    total_small = SmallSum(size, small_full, small_home, tail[0], tail[1], tail[2], tail[3:])

    mine = pltpu.make_async_copy(mixed_grad.at[row], head_grad.at[row], own_x)
    mine.start()
    swaps = []
    for k in range(1, number):
        there = (row + k) % number
        swaps.append(
            push(mixed_grad.at[there], head_grad.at[row], send_x.at[k], recv_x.at[k], ctx=there * split + lane)
        )
        swaps[-1].start()
    for home in early:
        home.start()

    steps = []
    for k in range(size):
        steps += [functools.partial(home.first, k) for home in early]
    for k in range(1, size):
        steps += [functools.partial(home.second, k) for home in early]
    steps += [functools.partial(home.second, 0, True) for home in early]

    def pump(count):
        for _ in range(min(count, len(steps))):
            steps.pop(0)()

    half = lax.broadcasted_iota(jnp.int32, (tile, 2 * HEAD_DIM), 1) < HEAD_DIM
    zero = jnp.zeros((tile, 2 * HEAD_DIM), WIDE)

    def prepare(i, _):
        rows = pl.ds(pl.multiple_of(i * tile, tile), tile)
        pair = key_value[rows].astype(WIDE)
        turned = pltpu.roll(pair, HEAD_DIM, 1)
        key_pad[0, rows] = jnp.where(half, pair, zero).astype(LOW)
        key_pad[1, rows] = jnp.where(half, zero, turned).astype(LOW)
        value_pad[0, rows] = jnp.where(half, turned, zero).astype(LOW)
        value_pad[1, rows] = jnp.where(half, zero, pair).astype(LOW)
        key_acc[rows] = zero
        value_acc[rows] = zero
        heads_grad[rows, pl.ds(0, 2 * HEAD_DIM)] = zero.astype(LOW)
        return 0

    lax.fori_loop(0, length // tile, prepare, 0)
    for k in range(1, number):
        here = (row + number - k) % number
        push(mixed_grad.at[here], head_grad.at[here], send_x.at[k], recv_x.at[k], ctx=here * split + lane).wait_recv()
    mine.wait()

    scale = HEAD_DIM**-0.5
    blocks = tile // tokens
    for i in range(number * tokens // tile):
        rows = pl.ds(i * tile, tile)
        query = query_pair[rows]
        grad = head_grad[pl.ds(i * blocks, blocks)].reshape(tile, 2 * HEAD_DIM)
        product = (grad.astype(WIDE) * out_pair[rows].astype(WIDE)).T
        deltas = [
            jnp.sum(product[h * HEAD_DIM : (h + 1) * HEAD_DIM], axis=0, keepdims=True) for h in range(GROUP)
        ]
        query_doc, query_place = docs_row[0:1, rows], places_row[0:1, rows]
        totals = [log_total[h : h + 1, rows] for h in range(GROUP)]
        query_acc[...] = zero

        def pairs(j, _):
            keys = pl.ds(pl.multiple_of(j * tile, tile), tile)
            place = lax.broadcasted_iota(jnp.int32, (tile, tile), 0) + j * tile
            allowed = (place <= query_place) & (docs_col[keys] == query_doc)
            key_part, value_part, query_part = zero, zero, zero
            for h in range(GROUP):
                mine_half = half if h == 0 else jnp.logical_not(half)
                score = dot_nt(key_pad[h, keys], query)
                prob = jnp.where(allowed, jnp.exp(score * scale - totals[h]), 0.0)
                slope = dot_nt(value_pad[h, keys], grad)
                ds = (prob * (slope - deltas[h])).astype(LOW)
                value_part = jnp.where(mine_half, dot_nn(prob.astype(LOW), grad), value_part)
                key_part = jnp.where(mine_half, dot_nn(ds, query), key_part)
                query_part = query_part + dot_tn(ds, key_pad[h, keys])
            key_acc[keys] += key_part
            value_acc[keys] += value_part
            query_acc[...] += query_part
            return 0

        lax.fori_loop(0, min(length // tile, (i + 1) * split), pairs, 0)
        turn = query_acc[...] * scale
        for b in range(blocks):
            at = pl.ds(pl.multiple_of(((i * blocks + b) * split + lane) * tokens, tokens), tokens)
            piece = turn[b * tokens : (b + 1) * tokens]
            heads_grad[at, pl.ds(0, 2 * HEAD_DIM)] = unturn(piece, cosine, sine, at, 0).astype(LOW)
        pump(9)

    def fold(i, _):
        rows = pl.ds(pl.multiple_of(i * tile, tile), tile)
        key_part, value_part = key_acc[rows], value_acc[rows]
        key_part = (key_part + pltpu.roll(key_part, HEAD_DIM, 1)) * scale
        value_part = value_part + pltpu.roll(value_part, HEAD_DIM, 1)
        both = jnp.where(half, key_part, value_part)
        heads_grad[rows, pl.ds(2 * HEAD_DIM, 2 * HEAD_DIM)] = unturn(both, cosine, sine, rows, 1).astype(LOW)
        return 0

    lax.fori_loop(0, length // tile, fold, 0)

    def transpose(i, _):
        rows = pl.ds(pl.multiple_of(i * tile, tile), tile)
        heads_turned[:, rows] = heads_grad[rows].astype(WIDE).T.astype(LOW)
        return 0

    lax.fori_loop(0, length // tile, transpose, 0)

    reduce = RingReduce(size, held, send_r, recv_r)
    small_full[...] = small[...]
    gain_row = small.shape[1] - 8

    def attend(place, slot):
        owner = ring_member(place, size)
        rows = pl.ds(pl.multiple_of(owner * tokens, tokens), tokens)
        part = dot_nt(heads_grad[rows], head_weight[...])
        attend_own[slot] = part.astype(LOW)
        normed = inputs_all[rows].astype(WIDE) * row_scale[rows]
        share = jnp.sum(part * normed, axis=0, keepdims=True)
        lanes = width // 4
        for s0 in range(4):
            small_full[s0, gain_row : gain_row + 1] += share[:, s0 * lanes : (s0 + 1) * lanes]

    place = ring_place(me, size)
    half_ring = size // 2
    attend(place + half_ring, 0)
    reduce.start(0, [attend_own.at[0]] * 2)
    for step in range(1, half_ring):
        attend(place + half_ring - step, 1)
        attend(place - half_ring + step, 2)
        if step == 1:
            def columns(j, _):
                cols = pl.ds(pl.multiple_of(j * tile, tile), tile)
                normed = inputs_all[:, cols].astype(WIDE) * row_scale[...]
                part = dot_nn(heads_turned[...], (normed * gain[gain.shape[0] - 8 : gain.shape[0] - 7, cols]).astype(LOW)).T.astype(LOW)
                depth = head_part.shape[1]
                head_part[pl.ds(j * (tile // depth), tile // depth)] = part.reshape(tile // depth, depth, HEAD_COLS)
                return 0

            lax.fori_loop(0, width // tile, columns, 0)
            late.start()
        reduce.start(step, [attend_own.at[1], attend_own.at[2]])
        pump(6)
    attend(place, 1)
    total_small.start()
    pump(len(steps))
    for k in range(size):
        late.first(k)
    total_small.middle()
    for k in range(1, size):
        late.second(k)
    late.second(0, True)
    reduce.finish(attend_sum, attend_own.at[1], attend_own.at[0])
    for home in early:
        home.close()
    late.close()
    total_small.finish()
    for copy in swaps:
        copy.wait_send()


def swap_halves(values):
    lane = lax.broadcasted_iota(jnp.int32, values.shape, 1) % HEAD_DIM
    return jnp.where(
        lane < HEAD_DIM // 2,
        pltpu.roll(values, values.shape[1] - HEAD_DIM // 2, 1),
        pltpu.roll(values, HEAD_DIM // 2, 1),
    )


def unturn(values, cosine, sine, rows, which):
    cos, sin = cosine[rows], sine[rows]
    if which:
        half = lax.broadcasted_iota(jnp.int32, values.shape, 1) < HEAD_DIM
        cos, sin = jnp.where(half, cos, 1.0), jnp.where(half, sin, 0.0)
    return values * cos - swap_halves(values) * sin


def attention_back(arrays, size, split, collective):
    (mixed_grad, gu_grads, down_grads, out_grads, small, query_pair, key_value, out_pair, log_total,
     docs_row, docs_col, places_row, cosine, sine, gain, inputs_all, row_scale, head_weight) = arrays
    tokens = mixed_grad.shape[1]
    length, width = inputs_all.shape
    tile = 2 * tokens
    blocks = [
        (gu_grads.shape[0],) + gu_grads.shape[2:], (down_grads.shape[0],) + down_grads.shape[2:],
        out_grads.shape[1:], (out_grads.shape[1], HEAD_COLS),
    ]
    small_rows = small.shape[1]
    dma = pltpu.SemaphoreType.DMA
    vmem = pl.BlockSpec(memory_space=pltpu.VMEM)
    anywhere = pl.BlockSpec(memory_space=pl.ANY)
    pair = (length, 2 * HEAD_DIM)
    scratch = [
        pltpu.VMEM(mixed_grad.shape, LOW),
        pltpu.VMEM((GROUP,) + pair, LOW), pltpu.VMEM((GROUP,) + pair, LOW),
        pltpu.VMEM(pair, WIDE), pltpu.VMEM(pair, WIDE), pltpu.VMEM((tile, 2 * HEAD_DIM), WIDE),
        pltpu.VMEM((length, HEAD_COLS), LOW), pltpu.VMEM((HEAD_COLS, length), LOW),
        pltpu.VMEM((4 * size, out_grads.shape[1], HEAD_COLS), LOW),
        pltpu.VMEM(small.shape, WIDE),
        pltpu.VMEM((3, tokens, width), LOW), pltpu.VMEM((2, size // 2, tokens, width), LOW),
        dma((2, size // 2)), dma((2, size // 2)), dma((size // split,)), dma((size // split,)), dma,
    ]
    for block in blocks:
        scratch += Homing.scratch(size, block)
    scratch += SmallSum.scratch(size, small_rows, width)
    return pl.pallas_call(
        functools.partial(back_kernel, size, split, tile),
        out_shape=[jax.ShapeDtypeStruct((tokens, width), WIDE)]
        + [jax.ShapeDtypeStruct((size,) + block, LOW) for block in blocks]
        + [jax.ShapeDtypeStruct((small_rows, width // 4), WIDE)],
        in_specs=[vmem, anywhere, anywhere, anywhere] + [vmem] * 14,
        out_specs=[vmem] * 6,
        scratch_shapes=scratch,
        compiler_params=pltpu.CompilerParams(
            collective_id=collective, has_side_effects=True, vmem_limit_bytes=62 << 20
        ),
        name="attention_back",
    )(*arrays)


def rms_scale(values):
    return lax.rsqrt(jnp.mean(values * values, axis=-1, keepdims=True) + NORM_EPS)


def rope_tables(places, factor):
    freqs = 1.0 / ROPE_BASE ** (jnp.arange(0, HEAD_DIM, 2).astype(WIDE) / HEAD_DIM)
    angles = (places.astype(WIDE) / factor)[None, :] * freqs[:, None]
    return jnp.cos(angles), jnp.sin(angles)


def dot(equation, left, right):
    return jnp.einsum(equation, left, right, preferred_element_type=WIDE)


def on_device(
    layer_input, document_ids, expert_routes, rope_factor, attention_gain, feedforward_gain,
    query_weight, key_weight, value_weight, output_weight, router_weight, gate_up, down_weight, cotangent,
):
    nseq, nctx = lax.axis_size("seq"), lax.axis_size("ctx")
    tokens, width = layer_input.shape[1:]
    length = tokens * nctx
    rows, experts, ff2 = gate_up.shape
    ff = ff2 // 2
    down_rows = down_weight.shape[0]
    per_unit = max(1, experts // nctx)
    ff_split = max(1, nctx // experts)
    ff_part = ff // ff_split
    head_split = nctx // KV_HEADS
    unit = lax.axis_index("ctx")
    owners = nseq * nctx

    if ff_split == 1:
        gu_pack = gate_up.astype(LOW).transpose(1, 0, 2).reshape(nctx, per_unit, rows, ff2)
    else:
        gu_pack = (
            gate_up.astype(LOW).reshape(rows, experts, 2, ff_split, ff_part).transpose(1, 3, 0, 2, 4)
            .reshape(nctx, per_unit, rows, 2 * ff_part)
        )
    down_pack = jnp.repeat(
        down_weight.astype(LOW).transpose(1, 0, 2), ff_split, axis=0
    ).reshape(nctx, per_unit, down_rows, width)
    head_pack = jnp.concatenate(
        [
            query_weight.reshape(rows, KV_HEADS, GROUP * HEAD_DIM),
            key_weight.reshape(rows, KV_HEADS, HEAD_DIM),
            value_weight.reshape(rows, KV_HEADS, HEAD_DIM),
        ],
        axis=-1,
    ).astype(LOW).transpose(1, 0, 2)
    head_pack = jnp.repeat(head_pack, head_split, axis=0)
    small_rows = experts + 8
    small_pack = jnp.concatenate(
        [router_weight, attention_gain[:, None], feedforward_gain[:, None], jnp.zeros((rows, 110 + 16 - experts), WIDE)],
        axis=1,
    ).astype(LOW)
    small_pack = jnp.broadcast_to(small_pack[None], (nctx,) + small_pack.shape)
    pack = jnp.concatenate([head_pack, small_pack], axis=2)
    documents = jnp.broadcast_to(document_ids.reshape(1, tokens), (8, tokens))
    cos_turned, sin_turned = rope_tables(jnp.arange(length, dtype=jnp.int32), rope_factor[0])

    (inputs_all, upstream_all, mixed_low, query_pair, key_value, out_pair, log_total, docs_row, docs_col, places_row,
     cosine, sine, row_scale, head_full, small_full, gu_full, down_full, out_full) = run_front(
        layer_input[0], cotangent[0], documents, cos_turned, sin_turned, pack, gu_pack, down_pack,
        output_weight.astype(LOW), head_split, owners, small_rows, 1,
    )
    gu_full = gu_full.reshape(per_unit, width, 2 * ff_part)
    down_full = down_full.reshape(per_unit, ff, width)
    if ff_split > 1:
        down_full = lax.dynamic_slice_in_dim(down_full, (unit % ff_split) * ff_part, ff_part, 1)
    out_full = out_full.reshape(HEADS * HEAD_DIM, width)
    router_full = small_full[:experts].astype(LOW)
    gain_one, gain_two = small_full[experts], small_full[experts + 1]

    inputs = layer_input[0].astype(WIDE)
    middle = inputs + dot("tj,jd->td", mixed_low, out_full)
    scale_two = rms_scale(middle)
    normed_two = middle * scale_two
    expert_input = (normed_two * gain_two).astype(LOW)
    logits = dot("td,ed->te", expert_input, router_full)
    chosen = jnp.any(
        expert_routes[0][:, :, None] == jnp.arange(experts, dtype=jnp.int32)[None, None, :], axis=1
    )
    picked = jnp.where(chosen, logits, NEG_BIG)
    expo_gate = jnp.where(chosen, jnp.exp(picked - jnp.max(picked, axis=-1, keepdims=True)), 0.0)
    combine = expo_gate / jnp.sum(expo_gate, axis=-1, keepdims=True)

    mix, back_sum, gate_grad_all, gu_grads, down_grads = run_experts(
        expert_input, combine.T, upstream_all, gu_full, down_full, nctx, ff_split, owners, down_rows, 3
    )

    layer_output = (middle + mix).astype(LOW)[None]
    upstream = cotangent[0].astype(WIDE)
    gate_grad = gate_grad_all[:, :per_unit].reshape(experts, ff_split, tokens).sum(axis=1).T
    gate_grad = jnp.where(chosen, gate_grad, 0.0)
    select_grad = combine * (gate_grad - jnp.sum(combine * gate_grad, axis=-1, keepdims=True))
    logit_grad = select_grad.astype(LOW)
    back_two = back_sum + dot("te,ed->td", logit_grad, router_full)
    router_part = dot("te,td->ed", logit_grad, expert_input)
    gain_two_part = jnp.sum(back_two * normed_two, axis=0)
    normed_two_grad = back_two * gain_two
    middle_grad = upstream + scale_two * (
        normed_two_grad - normed_two * jnp.mean(normed_two_grad * normed_two, axis=-1, keepdims=True)
    )
    project_grad = middle_grad.astype(LOW)
    out_grad_part = dot("tj,td->jd", mixed_low, project_grad)
    mixed_grad = dot("td,jd->tj", project_grad, out_full).astype(LOW)
    mixed_grad = mixed_grad.reshape(tokens, KV_HEADS, GROUP * HEAD_DIM).transpose(1, 0, 2)

    small_grads = jnp.concatenate(
        [router_part, gain_two_part[None], jnp.zeros((31 - experts, width), WIDE)], axis=0
    ).reshape(32, nseq, width // nseq).transpose(1, 0, 2)
    if ff_split > 1:
        down_grads = lax.dynamic_update_slice_in_dim(
            jnp.zeros((per_unit, owners, down_rows, width), LOW), down_grads,
            (unit % ff_split) * (ff_part // down_rows), 1,
        )
    attend_sum, gu_home, down_home, out_home, head_home, small_home = attention_back(
        [
            mixed_grad,
            gu_grads,
            down_grads,
            out_grad_part.astype(LOW).reshape(owners, rows, width),
            small_grads,
            query_pair, key_value, out_pair, log_total, docs_row, docs_col, places_row,
            cosine, sine, small_full, inputs_all.reshape(length, width), row_scale, head_full,
        ],
        nctx, head_split, 7,
    )
    gu_home, down_home = gu_home.astype(WIDE), down_home.astype(WIDE)
    out_home, head_home = out_home.astype(WIDE), head_home.astype(WIDE)
    gate_up_gradient = (
        gu_home.reshape(experts, ff_split, rows, 2, ff_part).transpose(2, 0, 3, 1, 4).reshape(rows, experts, ff2)
    )
    down_gradient = down_home.reshape(experts, ff_split, down_rows, width).sum(axis=1).transpose(1, 0, 2)
    output_gradient = out_home.sum(axis=0)
    head_home = head_home.reshape(KV_HEADS, head_split, rows, HEAD_COLS).sum(axis=1).transpose(1, 0, 2)
    query_gradient = head_home[..., : GROUP * HEAD_DIM].reshape(rows, HEADS * HEAD_DIM)
    key_gradient = head_home[..., GROUP * HEAD_DIM : -HEAD_DIM].reshape(rows, KV_HEADS * HEAD_DIM)
    value_gradient = head_home[..., -HEAD_DIM:].reshape(rows, KV_HEADS * HEAD_DIM)
    small_home = lax.dynamic_slice_in_dim(small_home, unit * rows, rows, axis=1)
    router_gradient = small_home[:experts].T

    scale_one = rms_scale(inputs)
    normed_one = inputs * scale_one
    normed_one_grad = attend_sum * gain_one
    input_gradient = (
        middle_grad
        + scale_one
        * (normed_one_grad - normed_one * jnp.mean(normed_one_grad * normed_one, axis=-1, keepdims=True))
    ).astype(LOW)[None]
    return (
        layer_output, input_gradient, small_home[24], small_home[experts],
        query_gradient, key_gradient, value_gradient, output_gradient, router_gradient,
        gate_up_gradient, down_gradient,
    )


def solution(mesh):
    both = ("seq", "ctx")
    return jax.shard_map(
        on_device,
        mesh=mesh,
        in_specs=(
            P("seq", "ctx", None), P("seq", "ctx"), P("seq", "ctx", None), P(), P(both), P(both),
            P(both, None), P(both, None), P(both, None), P(both, None), P(both, None),
            P(both, None, None), P(both, None, None), P("seq", "ctx", None),
        ),
        out_specs=(
            P("seq", "ctx", None), P("seq", "ctx", None), P(both), P(both),
            P(both, None), P(both, None), P(both, None), P(both, None), P(both, None),
            P(both, None, None), P(both, None, None),
        ),
        check_vma=False,
    )
```

profile of v0, /device:TPU:0, one launch (start us, length us, event | category | flops | bytes accessed | tf_op | source)
XLA Modules:
  0.0 360.1 jit_solution(17705224845618195741)
XLA Ops:
  1.3 1.2 multiply_sine_fusion
  2.6 1.8 convert_bitcast_fusion
  4.4 0.0 copy-start.16
  4.4 0.0 copy-start.17
  4.4 1.5 copy.56
  6.0 0.0 copy-done.7
  6.0 0.0 copy-start.15
  6.0 0.0 copy-start.20
  6.0 0.1 convert_bitcast_fusion.1
  6.1 1.1 copy.57
  7.2 0.1 reshape.161
  7.3 0.0 copy-start.3
  7.3 0.1 reshape.162
  7.5 0.1 maximum_bitcast_fusion
  7.6 0.1 copy.53
  7.7 0.1 copy.54
  7.8 0.1 copy.55
  7.9 0.1 pad.8.clone
  8.0 0.1 maximum_maximum_fusion
  8.1 0.7 pad_maximum_fusion.pack
  8.8 0.0 copy-done.15
  8.8 0.6 convert_element_type.68.out_rows
  9.5 0.6 broadcast_in_dim.51.docs_in
  10.1 120.8 %run_front.1 = (bf16[8,128,1024]{2,1,0:T(8,128)(2,1)}, bf16[8,128,1024]{2,1,0:T(8,128)(2,1)}, bf16[128,1024]{1,0:T(8,128)(2,1)}, bf16[1024,128]{1,0:T(8,128)(2,1...) custom-call(bf16[128,1024]{1,0:T(8,128)(2,1)} %bitcast.99, ...), custom_call_target="tpu_custom_call" | custom-call | tf_op jit(solution)/shard_map/run_front/pallas_call | solution.py:701
  130.9 0.0 copy-start.9
  130.9 0.0 copy-start.19
  130.9 2.3 multiply_reduce_fusion.2
  133.2 0.1 multiply_convert_fusion.expert_input
  133.3 0.0 copy-start.4
  133.4 0.7 copy-done.4
  134.0 0.2 fusion.20
  134.3 0.6 fusion.17.combine_rows
  134.9 85.0 %run_experts.1 = (f32[128,1024]{1,0:T(8,128)}, f32[128,1024]{1,0:T(8,128)}, f32[8,8,128]{2,1,0:T(8,128)}, bf16[2,32,32,1024]{3,2,1,0:T(8,128)(2,1)}, bf16[2,32,16,1024]{3,2,1,0:T(8,128)(2,1)}) custom-call(bf16[128,1024]{1,0:T(8,128)(2,1)} %copy-done.4, f32[16,128]{1,0:T(8,128)} %fusion.17.combine_rows, bf16[8,128,1024]{2,1,0:T(8,128)(2,1)} %get-tuple-element.43.upstream, ...), custom_call_target="tpu_custom_call" | custom-call | tf_op jit(solution)/shard_map/run_experts/pallas_call | solution.py:375
  219.9 0.0 copy-start.6
  219.9 0.8 slice.33
  220.8 1.1 fusion.23
  221.9 1.5 multiply_reduce_fusion
  223.4 0.1 pad.2.clone
  223.5 0.7 maximum_bitcast_fusion.1.small
  224.2 0.9 multiply_add_fusion
  225.2 2.1 convolution_convert_fusion
  227.2 0.0 copy-done
  227.2 0.8 convolution_convert_fusion.1
  228.0 0.2 copy.58
  228.2 0.9 copy.59
  229.1 111.8 %attention_back.1 = (f32[128,1024]{1,0:T(8,128)}, bf16[8,2,32,1024]{3,2,1,0:T(8,128)(2,1)}, bf16[8,2,16,1024]{3,2,1,0:T(8,128)(2,1)}, bf16[8,32,1024]{2,1,0:T(8,...) custom-call(bf16[8,128,128]{2,1,0:T(8,128)(2,1)} %bitcast.105, ...), custom_call_target="tpu_custom_call" | custom-call | tf_op jit(solution)/shard_map/attention_back/pallas_call | solution.py:1098
  340.9 3.1 reshape.181
  344.0 3.1 reshape.182
  347.1 4.2 %copy.66 = f32[32,16,1024]{2,1,0:T(8,128)} copy(f32[32,16,1024]{2,0,1:T(8,128)} %reshape.182) | data formatting | bytes 4194304 | tf_op jit(solution)/shard_map/reshape | solution.py:1244
  351.3 0.1 bitcast_convert_fusion
  351.5 1.6 copy.74
  353.0 0.0 copy-done.13
  353.1 0.1 fusion.21
  353.2 0.1 copy.62
  353.3 0.7 reshape.171
  354.0 0.1 copy.63
  354.1 0.7 reshape.172
  354.8 0.7 copy_bitcast_fusion.1
  355.5 0.1 fusion.7
  355.6 0.2 fusion.2
  355.8 0.9 fusion.9
  356.8 0.7 convert_reduce_fusion
  357.5 1.4 dynamic-slice_bitcast_fusion
  358.9 1.3 dynamic-slice_bitcast_fusion.1
  (56 shorter events, 0.3 us)
Async XLA Ops:
  2.6 3.4 copy-start.7
  4.4 2.8 copy-start.16
  4.4 2.9 copy-start.17
  6.0 1.5 copy-start.14
  6.0 1.6 copy-start.18
  6.0 1.7 copy-start.21
  6.0 1.8 copy-start.22
  6.0 2.8 copy-start.15
  6.0 3.5 copy-start.20
  7.3 123.6 %copy-start.3 = (bf16[1,128,1024]{2,1,0:T(8,128)(2,1)S(1)}, bf16[1,128,1024]{2,1,0:T(8,128)(2,1)}, u32[]{:S(2)}) copy-start(bf16[1,128,1024]{2,1,0:T(8,128)(2,1)} %param.14) | copy-start | bytes 786436
  130.9 2.3 copy-start.9
  130.9 2.4 copy-start.19
  133.3 0.7 copy-start.4
  219.9 4.3 %copy-start.6 = (bf16[1,128,1024]{2,1,0:T(8,128)(2,1)S(1)}, bf16[1,128,1024]{2,1,0:T(8,128)(2,1)}, u32[]{:S(2)}) copy-start(bf16[1,128,1024]{2,1,0:T(8,128)(2,1)} %param.27) | copy-start | bytes 786436
  219.9 4.3 %copy-start.10 = (f32[128,1024]{1,0:T(8,128)S(1)}, f32[128,1024]{1,0:T(8,128)}, u32[]{:S(2)}) copy-start(f32[128,1024]{1,0:T(8,128)} %get-tuple-element.46) | copy-start | bytes 1572868
  221.9 3.3 copy-start.8
  225.2 2.1 copy-start.1
  225.2 2.1 copy-start
  347.1 4.2 %copy-start.11 = (bf16[8,2,16,1024]{3,2,1,0:T(8,128)(2,1)S(1)}, bf16[8,2,16,1024]{3,2,1,0:T(8,128)(2,1)}, u32[]{:S(2)}) copy-start(bf16[8,2,16,1024]{3,2,1,0:T(8,128)(2,1)} %get-tuple-element.68) | copy-start | bytes 1572868
  351.3 1.8 copy-start.13
  351.4 4.2 %copy-start.5 = (f32[128,1024]{1,0:T(8,128)S(1)}, f32[128,1024]{1,0:T(8,128)}, u32[]{:S(2)}) copy-start(f32[128,1024]{1,0:T(8,128)} %get-tuple-element.63) | copy-start | bytes 1572868
  353.0 2.8 copy-start.2
  353.1 3.7 %copy-start.12 = (bf16[8,32,1024]{2,1,0:T(8,128)(2,1)S(1)}, bf16[8,32,1024]{2,1,0:T(8,128)(2,1)}, u32[]{:S(2)}) copy-start(bf16[8,32,1024]{2,1,0:T(8,128)(2,1)} %get-tuple-element.66) | copy-start | bytes 1572868
where the time goes:
time: 361 us; the launch traced here: 360 us
  Pallas kernels  318 us (88%)
  local copies, waits for them, and re-layouts  23.6 us (7%)
  other arithmetic  9.41 us (3%)
  matrix products  7.89 us (2%)
    pallas_call x1, Pallas kernels, run_front(): pl.pallas_call(functools.partial(front_kernel, size, split, tile), out_sh...  121 us
    pallas_call x1, Pallas kernels, attention_back(): pl.pallas_call(functools.partial(back_kernel, size, split, tile), out_sha...  112 us
    pallas_call x1, Pallas kernels, run_experts(): pl.pallas_call(functools.partial(expert_kernel, size, split), out_shape=[...  85 us
    reshape x3, local copies, waits for them, and re-layouts, on_device(): gu_home.reshape(experts, ff_split, rows, 2, ff_part)  10.4 us
    dot_general x6, matrix products, dot(): return jnp.einsum(equation, left, right, preferred_element_type=WIDE)  7.89 us

commit v1 on v0

--- a/solution.py
+++ b/solution.py
@@ -39,6 +39,16 @@
     if abs(distance) == size // 2:
         return 1
     return 2 * abs(distance) + (distance > 0)
+
+
+def slot_seen(owner, viewer, size):
+    half = size // 2
+    ahead = (ring_place(owner, size) - ring_place(viewer, size) + 2 * size) % size
+    far = ahead // half
+    plain = (2 * ahead + 1) * (1 - far) + 2 * (size - ahead) * far
+    same = (size - ahead) // size
+    opposite = (size - (ahead + half) % size) // size
+    return plain - same - (size - 1) * opposite
 
 
 def core_mate(index):
@@ -106,6 +116,72 @@
     def finish(self):
         self.land()
         self.drain()
+
+
+class LineGather:
+    def __init__(self, size, source, slab, sems):
+        self.source, self.slab, self.count = source, slab, size // 2
+        self.send, self.recv, self.send_m, self.recv_m = sems
+        self.me = lax.axis_index("ctx")
+        self.spot, self.side = self.me // 2, self.me % 2
+        self.mate = core_mate(self.me)
+
+    def _line(self, way, step):
+        owner = self.me - 2 * step if way == 0 else self.me + 2 * step
+        there = self.me + 2 if way == 0 else self.me - 2
+        source = self.slab(owner, self.me) if step else self.source
+        return push(source, self.slab(owner, there), self.send.at[way, step], self.recv.at[way, step], ctx=there)
+
+    def _arriving(self, way, step):
+        owner = self.me - 2 * step - 2 if way == 0 else self.me + 2 * step + 2
+        here = self.slab(owner, self.me)
+        return push(here, here, self.send.at[way, step], self.recv.at[way, step], ctx=self.mate)
+
+    def _across(self, spot, own=False):
+        owner = 2 * spot + self.side
+        source = self.source if own else self.slab(owner, self.me)
+        return push(
+            source, self.slab(owner, self.mate), self.send_m.at[spot], self.recv_m.at[spot], ctx=self.mate
+        )
+
+    def _sends(self, way, step):
+        if way == 0:
+            return (self.spot + 1 < self.count) & (self.spot >= step)
+        return (self.spot >= 1) & (self.spot + step < self.count)
+
+    def start(self):
+        for way in range(2):
+            pl.when(self._sends(way, 0))(self._line(way, 0).start)
+        self._across(self.spot, True).start()
+
+    def turn(self, step):
+        for way in range(2):
+            there = self.spot >= step if way == 0 else self.spot + step < self.count
+
+            @pl.when(there)
+            def _():
+                self._arriving(way, step - 1).wait_recv()
+                self._across(self.spot - step if way == 0 else self.spot + step).start()
+
+            pl.when(self._sends(way, step))(self._line(way, step).start)
+
+    def finish(self):
+        for spot in range(self.count):
+            owner = 2 * spot + 1 - self.side
+            here = self.slab(owner, self.me)
+            push(here, here, self.send_m.at[spot], self.recv_m.at[spot], ctx=self.mate).wait_recv()
+
+    def drain(self):
+        for spot in range(self.count):
+            self._across(spot).wait_send()
+        for way in range(2):
+            for step in range(self.count - 1):
+                pl.when(self._sends(way, step))(self._line(way, step).wait_send)
+
+    @staticmethod
+    def scratch(size):
+        dma, count = pltpu.SemaphoreType.DMA, size // 2
+        return [dma((2, count)), dma((2, count)), dma((count,)), dma((count,))]
 
 
 def row_step(rows):
@@ -409,8 +485,8 @@
 
 
 class Spread:
-    def __init__(self, size, source, slab, sems):
-        self.size, self.source, self.slab = size, source, slab
+    def __init__(self, size, source, slab, sems, gathered=False):
+        self.size, self.source, self.slab, self.gathered = size, source, slab, gathered
         self.send_a, self.recv_a, self.send_b, self.recv_b, self.own = sems
         self.me, self.seq = lax.axis_index("ctx"), lax.axis_index("seq")
 
@@ -448,11 +524,11 @@
     def step(self, k):
         if k == 0:
             self.local().wait()
-        else:
+        elif not self.gathered:
             self.inward(k).wait_recv()
         self.sideways(1, k).start()
         self.sideways(0, k).start()
-        if k:
+        if k and not self.gathered:
             self.pass_on(k - 1)
 
     def pass_on(self, k):
@@ -468,7 +544,7 @@
         for k in range(self.size):
             for which in range(3):
                 self.sideways(which, k).wait_send()
-            if k:
+            if k and not self.gathered:
                 self.outward(k).wait_send()
 
     @staticmethod
@@ -483,7 +559,7 @@
     inputs_all, upstream_all, mixed, query_pair, key_value, out_pair, log_total, docs_row, docs_col, places_row,
     cosine, sine, row_scale, head_weight, small, gu_full, down_full, out_full,
     docs_all, pack_all, key_pad, value_turned, head_out,
-    send_t, recv_t, send_u, recv_u, send_n, recv_n, send_x, recv_x, own, *scratch,
+    send_t, recv_t, send_n, recv_n, send_x, recv_x, own, *scratch,
 ):
     me, seq = lax.axis_index("ctx"), lax.axis_index("seq")
     lane, row, number = me % split, me // split, size // split
@@ -498,10 +574,15 @@
     bulk = [
         Spread(size, lambda c: gu_pack.at[c], lambda owner: gu_full.at[:, owner], scratch[5:10]),
         Spread(size, lambda c: down_pack.at[c], lambda owner: down_full.at[:, owner], scratch[10:15]),
-        Spread(size, lambda c: out_rows, lambda owner: out_full.at[owner], scratch[15:20]),
     ]
+    out = Spread(size, lambda c: out_rows, lambda owner: out_full.at[owner], scratch[15:20], True)
+    lines = LineGather(
+        size, out_rows, lambda owner, viewer: out_full.at[seq * size + owner], scratch[20:24]
+    )
     ring = RingGather(size, tokens_in, inputs_all, send_t, recv_t)
-    ring_up = RingGather(size, upstream, upstream_all, send_u, recv_u, True)
+    lines_up = LineGather(
+        size, upstream, lambda owner, viewer: upstream_all.at[slot_seen(owner, viewer, size)], scratch[24:28]
+    )
 
     def note(k):
         return push(docs_in, docs_all.at[me], send_n.at[k], recv_n.at[k], ctx=(me + k) % size)
@@ -510,9 +591,15 @@
         here = (me + size - k) % size
         return push(docs_in, docs_all.at[here], send_n.at[k], recv_n.at[k], ctx=here)
 
+    def send_bulk(turn):
+        for k in range(2 * turn + 1, min(2 * turn + 3, size)):
+            for part in bulk:
+                part.outward(k).start()
+
     heads.start()
     for k in range(1, size):
         note(k).start()
+    lines.start()
     ring.start(0)
     heads.local().start()
     local = [
@@ -521,7 +608,7 @@
     ]
     for copy in local:
         copy.start()
-    for part in bulk:
+    for part in bulk + [out]:
         part.local().start()
     docs_all[me] = docs_in[...]
 
@@ -536,9 +623,11 @@
     for k in range(size):
         heads.step(k)
     heads.pass_on(size - 1)
-    for part in bulk:
+    for part in bulk + [out]:
         part.step(0)
+    lines.turn(1)
     ring.start(1)
+    send_bulk(0)
     for k in range(1, size):
         noted(k).wait_recv()
     log_total[...] = jnp.zeros_like(log_total)
@@ -597,10 +686,18 @@
             def _():
                 if step > 1:
                     ring.start(step)
+                if step < steps - 1:
+                    lines.turn(step + 1)
+                else:
+                    lines.finish()
+                    for k in range(1, size):
+                        out.step(k)
+                send_bulk(step)
                 if step == steps - 1:
-                    ring_up.start(0)
-                    for part in bulk:
-                        part.start()
+                    lines_up.start()
+                for k in range(2 * step - 3, 2 * step - 1):
+                    for part in bulk if k > 0 else []:
+                        part.step(k)
 
         def side(way, _):
             project(place + (2 * way - 1) * turn)
@@ -612,11 +709,13 @@
     ring.land()
     project(place + steps)
 
-    todo = []
-    for k in range(1, size):
+    todo = [functools.partial(out.pass_on, k) for k in range(size)]
+    todo.append(functools.partial(lines_up.turn, 1))
+    for k in range(size - 3, size):
         todo += [functools.partial(part.step, k) for part in bulk]
-        if k % 2 == 0 and k // 2 < steps:
-            todo.append(functools.partial(ring_up.start, k // 2))
+        if k < size - 1:
+            todo.append(functools.partial(lines_up.turn, k - size + 5))
+    todo += [functools.partial(lines_up.turn, k) for k in range(4, steps)]
 
     def pump(count):
         for _ in range(min(count, len(todo))):
@@ -654,7 +753,7 @@
         out_pair[rows] = result
         blocks = tile // tokens
         head_out[pl.ds(i * blocks, blocks)] = result.astype(LOW).reshape(blocks, tokens, 2 * HEAD_DIM)
-        pump(3)
+        pump(4)
 
     def seat(index):
         return mixed.at[:, pl.ds(pl.multiple_of(index * 2 * HEAD_DIM, 2 * HEAD_DIM), 2 * HEAD_DIM)]
@@ -669,20 +768,21 @@
     pump(len(todo))
     for part in bulk:
         part.pass_on(size - 1)
-    ring_up.land()
+    lines_up.finish()
     for k in range(1, number):
         here = (row + number - k) % number
         push(head_out.at[here], seat(here), send_x.at[k], recv_x.at[k], ctx=here * split + lane).wait_recv()
     mine.wait()
-    for part in bulk:
+    for part in bulk + [out]:
         part.land()
     for copy in swaps:
         copy.wait_send()
     for k in range(1, size):
         note(k).wait_send()
     ring.drain()
-    ring_up.drain()
-    for part in [heads] + bulk:
+    lines.drain()
+    lines_up.drain()
+    for part in [heads, out] + bulk:
         part.drain()
 
 
@@ -719,9 +819,9 @@
             pltpu.VMEM((GROUP, length, pair), LOW),
             pltpu.VMEM((HEAD_DIM, length), LOW),
             pltpu.VMEM((size // split, tokens, pair), LOW),
-            dma((2, size // 2)), dma((2, size // 2)), dma((2, size // 2)), dma((2, size // 2)),
+            dma((2, size // 2)), dma((2, size // 2)),
             dma((size,)), dma((size,)), dma((size // split,)), dma((size // split,)), dma((3,)),
-        ] + Spread.scratch(size) * 4,
+        ] + Spread.scratch(size) * 4 + LineGather.scratch(size) * 2,
         compiler_params=pltpu.CompilerParams(
             collective_id=collective, has_side_effects=True, vmem_limit_bytes=60 << 20
         ),
@@ -977,7 +1077,7 @@
             at = pl.ds(pl.multiple_of(((i * blocks + b) * split + lane) * tokens, tokens), tokens)
             piece = turn[b * tokens : (b + 1) * tokens]
             heads_grad[at, pl.ds(0, 2 * HEAD_DIM)] = unturn(piece, cosine, sine, at, 0).astype(LOW)
-        pump(9)
+        pump(6)
 
     def fold(i, _):
         rows = pl.ds(pl.multiple_of(i * tile, tile), tile)
@@ -1031,7 +1131,7 @@
             lax.fori_loop(0, width // tile, columns, 0)
             late.start()
         reduce.start(step, [attend_own.at[1], attend_own.at[2]])
-        pump(6)
+        pump(3)
     attend(place, 1)
     total_small.start()
     pump(len(steps))
@@ -1240,10 +1340,14 @@
     )
     gu_home, down_home = gu_home.astype(WIDE), down_home.astype(WIDE)
     out_home, head_home = out_home.astype(WIDE), head_home.astype(WIDE)
-    gate_up_gradient = (
-        gu_home.reshape(experts, ff_split, rows, 2, ff_part).transpose(2, 0, 3, 1, 4).reshape(rows, experts, ff2)
-    )
-    down_gradient = down_home.reshape(experts, ff_split, down_rows, width).sum(axis=1).transpose(1, 0, 2)
+    if ff_split == 1:
+        gate_up_gradient = gu_home.reshape(experts, rows, ff2).transpose(1, 0, 2)
+        down_gradient = down_home.reshape(experts, down_rows, width).transpose(1, 0, 2)
+    else:
+        gate_up_gradient = (
+            gu_home.reshape(experts, ff_split, rows, 2, ff_part).transpose(2, 0, 3, 1, 4).reshape(rows, experts, ff2)
+        )
+        down_gradient = down_home.reshape(experts, ff_split, down_rows, width).sum(axis=1).transpose(1, 0, 2)
     output_gradient = out_home.sum(axis=0)
     head_home = head_home.reshape(KV_HEADS, head_split, rows, HEAD_COLS).sum(axis=1).transpose(1, 0, 2)
     query_gradient = head_home[..., : GROUP * HEAD_DIM].reshape(rows, HEADS * HEAD_DIM)

time: 361 us -> 333 us (0.922)
  Pallas kernels: 318 us -> 297 us
  local copies, waits for them, and re-layouts: 23.6 us -> 15.7 us
    reshape x3 -> x0, local copies, waits for them, and re-layouts: 10.4 us -> none  [on_device(): gu_home.reshape(experts, ff_split, rows, 2, ff_part)]
    pallas_call x1, Pallas kernels: 112 us -> 103 us  [attention_back(): pl.pallas_call(functools.partial(back_kernel, size, split, tile), out_sha...]
    pallas_call x1, Pallas kernels: 85 us -> 78.3 us  [run_experts(): pl.pallas_call(functools.partial(expert_kernel, size, split), out_shape=[...]
    pallas_call x1, Pallas kernels: 121 us -> 115 us  [run_front(): pl.pallas_call(functools.partial(front_kernel, size, split, tile), out_sh...]
where the time goes in v1:
time: 333 us
  Pallas kernels  297 us (89%)
  local copies, waits for them, and re-layouts  15.7 us (5%)
  other arithmetic  10.9 us (3%)
  matrix products  7.91 us (2%)
    pallas_call x1, Pallas kernels, run_front(): pl.pallas_call(functools.partial(front_kernel, size, split, tile), out_sh...  115 us
    pallas_call x1, Pallas kernels, attention_back(): pl.pallas_call(functools.partial(back_kernel, size, split, tile), out_sha...  103 us
    pallas_call x1, Pallas kernels, run_experts(): pl.pallas_call(functools.partial(expert_kernel, size, split), out_shape=[...  78.3 us
    dot_general x6, matrix products, dot(): return jnp.einsum(equation, left, right, preferred_element_type=WIDE)  7.91 us

profile of v1, /device:TPU:0, one launch (start us, length us, event | category | flops | bytes accessed | tf_op | source)
XLA Modules:
  0.0 332.8 jit_solution(5821627547784964889)
XLA Ops:
  1.3 1.2 multiply_sine_fusion
  2.6 1.8 convert_bitcast_fusion
  4.4 0.0 copy-start.14
  4.4 0.0 copy-start.15
  4.4 1.5 copy.56
  6.0 0.0 copy-done.5
  6.0 0.0 copy-start.13
  6.0 0.0 copy-start.18
  6.0 0.1 convert_bitcast_fusion.1
  6.1 1.1 copy.57
  7.2 0.0 copy-done.14
  7.2 0.1 reshape.155
  7.3 0.0 copy-done.15
  7.3 0.0 copy-start.1
  7.3 0.1 reshape.156
  7.5 0.0 copy-done.12
  7.5 0.1 maximum_bitcast_fusion
  7.6 0.1 copy.53
  7.7 0.1 copy.54
  7.8 0.1 copy.55
  7.9 0.1 pad.8.clone
  8.0 0.1 maximum_maximum_fusion
  8.1 0.7 pad_maximum_fusion.pack
  8.8 0.6 convert_element_type.68.out_rows
  9.5 0.6 broadcast_in_dim.51.docs_in
  10.1 115.2 %run_front.1 = (bf16[8,128,1024]{2,1,0:T(8,128)(2,1)}, bf16[8,128,1024]{2,1,0:T(8,128)(2,1)}, bf16[128,1024]{1,0:T(8,128)(2,1)}, bf16[1024,128]{1,0:T(8,128)(2,1...) custom-call(bf16[128,1024]{1,0:T(8,128)(2,1)} %bitcast.99, ...), custom_call_target="tpu_custom_call" | custom-call | tf_op jit(solution)/shard_map/run_front/pallas_call | solution.py:801
  125.3 0.0 copy-start.17
  125.3 2.3 multiply_reduce_fusion.2
  127.6 0.1 multiply_convert_fusion.expert_input
  127.7 0.0 copy-start.2
  127.7 0.7 copy-done.2
  128.4 0.2 fusion.20
  128.6 0.6 fusion.17.combine_rows
  129.2 78.3 %run_experts.1 = (f32[128,1024]{1,0:T(8,128)}, f32[128,1024]{1,0:T(8,128)}, f32[8,8,128]{2,1,0:T(8,128)}, bf16[2,32,32,1024]{3,2,1,0:T(8,128)(2,1)}, bf16[2,32,16,1024]{3,2,1,0:T(8,128)(2,1)}) custom-call(bf16[128,1024]{1,0:T(8,128)(2,1)} %copy-done.2, f32[16,128]{1,0:T(8,128)} %fusion.17.combine_rows, bf16[8,128,1024]{2,1,0:T(8,128)(2,1)} %get-tuple-element.43.upstream, ...), custom_call_target="tpu_custom_call" | custom-call | tf_op jit(solution)/shard_map/run_experts/pallas_call | solution.py:451
  207.5 0.0 copy-start.4
  207.5 0.8 slice.33
  208.4 1.1 fusion.23
  209.5 1.5 multiply_reduce_fusion
  211.0 0.1 pad.2.clone
  211.1 0.7 maximum_bitcast_fusion.1.small
  211.8 0.9 multiply_add_fusion
  212.8 2.1 convolution_convert_fusion
  214.8 0.8 convolution_convert_fusion.1
  215.7 0.2 copy.58
  215.9 0.9 copy.59
  216.7 103.2 %attention_back.1 = (f32[128,1024]{1,0:T(8,128)}, bf16[8,2,32,1024]{3,2,1,0:T(8,128)(2,1)}, bf16[8,2,16,1024]{3,2,1,0:T(8,128)(2,1)}, bf16[8,32,1024]{2,1,0:T(8,...) custom-call(bf16[8,128,128]{2,1,0:T(8,128)(2,1)} %bitcast.106, ...), custom_call_target="tpu_custom_call" | custom-call | tf_op jit(solution)/shard_map/attention_back/pallas_call | solution.py:1198
  319.9 1.5 bitcast_convert_fusion
  321.4 0.0 copy-start.9
  321.4 2.5 copy.74
  323.9 0.1 bitcast_convert_fusion.1
  324.1 1.6 copy.75
  325.7 0.1 fusion.21
  325.8 0.1 copy.62
  325.9 0.7 reshape.165
  326.6 0.1 copy.63
  326.7 0.7 reshape.166
  327.4 0.7 copy_bitcast_fusion.2
  328.1 0.1 fusion.7
  328.2 0.0 copy-done.3
  328.2 0.2 fusion.2
  328.5 0.9 fusion.9
  329.4 0.7 convert_reduce_fusion
  330.1 1.4 dynamic-slice_bitcast_fusion
  331.5 1.3 dynamic-slice_bitcast_fusion.1
  (51 shorter events, 0.3 us)
Async XLA Ops:
  2.6 3.4 %copy-start.5 = (f32[16,16,1024]{2,1,0:T(8,128)S(1)}, f32[16,16,1024]{2,1,0:T(8,128)}, u32[]{:S(2)}) copy-start(f32[16,16,1024]{2,1,0:T(8,128)} %param.26) | copy-start | bytes 3145732
  4.4 2.8 copy-start.14
  4.4 2.9 copy-start.15
  6.0 1.5 copy-start.12
  6.0 1.6 copy-start.16
  6.0 1.7 copy-start.19
  6.0 1.8 copy-start.20
  6.0 2.8 copy-start.13
  6.0 3.5 %copy-start.18 = (s32[1,128]{1,0:T(1,128)S(1)}, s32[1,128]{1,0:T(1,128)}, u32[]{:S(2)}) copy-start(s32[1,128]{1,0:T(1,128)} %param.15) | copy-start | bytes 1540
  7.3 118.0 %copy-start.1 = (bf16[1,128,1024]{2,1,0:T(8,128)(2,1)S(1)}, bf16[1,128,1024]{2,1,0:T(8,128)(2,1)}, u32[]{:S(2)}) copy-start(bf16[1,128,1024]{2,1,0:T(8,128)(2,1)} %param.14) | copy-start | bytes 786436
  125.2 2.3 copy-start.7
  125.3 2.4 copy-start.17
  127.7 0.7 copy-start.2
  207.5 4.3 %copy-start.4 = (bf16[1,128,1024]{2,1,0:T(8,128)(2,1)S(1)}, bf16[1,128,1024]{2,1,0:T(8,128)(2,1)}, u32[]{:S(2)}) copy-start(bf16[1,128,1024]{2,1,0:T(8,128)(2,1)} %param.27) | copy-start | bytes 786436
  207.5 4.3 %copy-start.8 = (f32[128,1024]{1,0:T(8,128)S(1)}, f32[128,1024]{1,0:T(8,128)}, u32[]{:S(2)}) copy-start(f32[128,1024]{1,0:T(8,128)} %get-tuple-element.46) | copy-start | bytes 1572868
  209.5 3.3 copy-start.6
  212.8 2.1 copy-start
  321.4 2.6 copy-start.9
  323.9 1.7 copy-start.11
  324.1 4.1 %copy-start.3 = (f32[128,1024]{1,0:T(8,128)S(1)}, f32[128,1024]{1,0:T(8,128)}, u32[]{:S(2)}) copy-start(f32[128,1024]{1,0:T(8,128)} %get-tuple-element.63) | copy-start | bytes 1572868
  325.7 3.7 %copy-start.10 = (bf16[8,32,1024]{2,1,0:T(8,128)(2,1)S(1)}, bf16[8,32,1024]{2,1,0:T(8,128)(2,1)}, u32[]{:S(2)}) copy-start(bf16[8,32,1024]{2,1,0:T(8,128)(2,1)} %get-tuple-element.66) | copy-start | bytes 1572868

commit v2 on v1

--- a/solution.py
+++ b/solution.py
@@ -85,10 +85,10 @@
         self.right, self.left = ring_peers(size)
         self.steps = size // 2
 
-    def _copy(self, way, step, arriving):
+    def _copy(self, way, step, piece, arriving):
         sign = 2 * way - 1
         rows = self.source.shape[0]
-        part = pl.ds(way * (rows // 2), rows // 2) if step == self.steps - 1 else pl.ds(0, rows)
+        part = pl.ds(piece * (rows // 2), rows // 2)
         if self.relative:
             here, there = slot_of(sign * step, self.size), slot_of(sign * (step + 1), self.size)
         else:
@@ -96,22 +96,26 @@
         dst = self.target.at[there, part]
         src = self.target.at[here, part] if step else self.source.at[part]
         where = self.left if way else self.right
-        return push(dst if arriving else src, dst, self.send.at[way, step], self.recv.at[way, step], ctx=where)
+        send, recv = self.send.at[way, step, piece], self.recv.at[way, step, piece]
+        return push(dst if arriving else src, dst, send, recv, ctx=where)
 
     def start(self, step):
-        for way in range(2):
-            if step:
-                self._copy(way, step - 1, 1).wait_recv()
-            self._copy(way, step, 0).start()
+        for piece in range(2):
+            for way in range(2):
+                if step:
+                    self._copy(way, step - 1, piece, 1).wait_recv()
+                if step < self.steps - 1 or piece == way:
+                    self._copy(way, step, piece, 0).start()
 
     def land(self):
         for way in range(2):
-            self._copy(way, self.steps - 1, 1).wait_recv()
+            self._copy(way, self.steps - 1, way, 1).wait_recv()
 
     def drain(self):
         for way in range(2):
             for step in range(self.steps):
-                self._copy(way, step, 0).wait_send()
+                for piece in range(2) if step < self.steps - 1 else [way]:
+                    self._copy(way, step, piece, 0).wait_send()
 
     def finish(self):
         self.land()
@@ -474,7 +478,8 @@
             pltpu.VMEM((size, 8, tokens), WIDE),
             pltpu.VMEM((2, size // 2, tokens, width), LOW),
             pltpu.VMEM((2, size // 2, tokens, width), LOW),
-            dma(steps), dma(steps), dma(steps), dma(steps), dma(steps), dma(steps), dma(steps), dma(steps),
+            dma(steps + (2,)), dma(steps + (2,)), dma(steps + (2,)), dma(steps + (2,)),
+            dma(steps), dma(steps), dma(steps), dma(steps),
             dma((size,)), dma((size,)), dma((4,)),
         ],
         compiler_params=pltpu.CompilerParams(
@@ -819,7 +824,7 @@
             pltpu.VMEM((GROUP, length, pair), LOW),
             pltpu.VMEM((HEAD_DIM, length), LOW),
             pltpu.VMEM((size // split, tokens, pair), LOW),
-            dma((2, size // 2)), dma((2, size // 2)),
+            dma((2, size // 2, 2)), dma((2, size // 2, 2)),
             dma((size,)), dma((size,)), dma((size // split,)), dma((size // split,)), dma((3,)),
         ] + Spread.scratch(size) * 4 + LineGather.scratch(size) * 2,
         compiler_params=pltpu.CompilerParams(
@@ -969,16 +974,20 @@
 
 def back_kernel(
     size, split, tile,
-    mixed_grad, gu_grads, down_grads, out_grads, small, query_pair, key_value, out_pair, log_total,
+    mixed_grad, gu_grads, down_grads, mixed_low, project_grad, small, query_pair, key_value, out_pair, log_total,
     docs_row, docs_col, places_row, cosine, sine, gain, inputs_all, row_scale, head_weight,
     attend_sum, gu_home, down_home, out_home, head_home, small_home,
     head_grad, key_pad, value_pad, key_acc, value_acc, query_acc, heads_grad, heads_turned, head_part, small_full,
-    attend_own, held, send_r, recv_r, send_x, recv_x, own_x, *scratch,
+    attend_own, held, out_grads, send_r, recv_r, send_x, recv_x, own_x, *scratch,
 ):
     me, seq = lax.axis_index("ctx"), lax.axis_index("seq")
     lane, row, number = me % split, me // split, size // split
-    tokens = mixed_grad.shape[1]
+    tokens = mixed_grad.shape[0]
     length, width = inputs_all.shape
+
+    def heads_of(index):
+        return mixed_grad.at[:, pl.ds(pl.multiple_of(index * 2 * HEAD_DIM, 2 * HEAD_DIM), 2 * HEAD_DIM)]
+
     greet(
         [{"ctx": (me + k) % size} for k in range(1, size)]
         + [{"seq": (seq + k) % 4} for k in range(1, 4)]
@@ -993,17 +1002,27 @@
     tail = scratch[48:]
     total_small = SmallSum(size, small_full, small_home, tail[0], tail[1], tail[2], tail[3:])
 
-    mine = pltpu.make_async_copy(mixed_grad.at[row], head_grad.at[row], own_x)
+    mine = pltpu.make_async_copy(heads_of(row), head_grad.at[row], own_x)
     mine.start()
     swaps = []
     for k in range(1, number):
         there = (row + k) % number
         swaps.append(
-            push(mixed_grad.at[there], head_grad.at[row], send_x.at[k], recv_x.at[k], ctx=there * split + lane)
+            push(heads_of(there), head_grad.at[row], send_x.at[k], recv_x.at[k], ctx=there * split + lane)
         )
         swaps[-1].start()
-    for home in early:
+    for home in early[:2]:
         home.start()
+
+    def out_tile(j, _):
+        cols = pl.ds(pl.multiple_of(j * tile, tile), tile)
+        depth = out_grads.shape[1]
+        part = dot_tn(mixed_low[:, cols], project_grad[...]).reshape(tile // depth, depth, width)
+        out_grads[pl.ds(j * (tile // depth), tile // depth)] = part.astype(LOW)
+        return 0
+
+    lax.fori_loop(0, width // tile, out_tile, 0)
+    early[2].start()
 
     steps = []
     for k in range(size):
@@ -1035,7 +1054,7 @@
     lax.fori_loop(0, length // tile, prepare, 0)
     for k in range(1, number):
         here = (row + number - k) % number
-        push(mixed_grad.at[here], head_grad.at[here], send_x.at[k], recv_x.at[k], ctx=here * split + lane).wait_recv()
+        push(heads_of(here), head_grad.at[here], send_x.at[k], recv_x.at[k], ctx=here * split + lane).wait_recv()
     mine.wait()
 
     scale = HEAD_DIM**-0.5
@@ -1134,9 +1153,9 @@
         pump(3)
     attend(place, 1)
     total_small.start()
-    pump(len(steps))
     for k in range(size):
         late.first(k)
+    pump(len(steps))
     total_small.middle()
     for k in range(1, size):
         late.second(k)
@@ -1168,14 +1187,15 @@
 
 
 def attention_back(arrays, size, split, collective):
-    (mixed_grad, gu_grads, down_grads, out_grads, small, query_pair, key_value, out_pair, log_total,
+    (mixed_grad, gu_grads, down_grads, mixed_low, project_grad, small, query_pair, key_value, out_pair, log_total,
      docs_row, docs_col, places_row, cosine, sine, gain, inputs_all, row_scale, head_weight) = arrays
-    tokens = mixed_grad.shape[1]
+    tokens = mixed_grad.shape[0]
     length, width = inputs_all.shape
     tile = 2 * tokens
+    out_shape = (4 * size, gu_grads.shape[2], width)
     blocks = [
         (gu_grads.shape[0],) + gu_grads.shape[2:], (down_grads.shape[0],) + down_grads.shape[2:],
-        out_grads.shape[1:], (out_grads.shape[1], HEAD_COLS),
+        out_shape[1:], (out_shape[1], HEAD_COLS),
     ]
     small_rows = small.shape[1]
     dma = pltpu.SemaphoreType.DMA
@@ -1183,13 +1203,14 @@
     anywhere = pl.BlockSpec(memory_space=pl.ANY)
     pair = (length, 2 * HEAD_DIM)
     scratch = [
-        pltpu.VMEM(mixed_grad.shape, LOW),
+        pltpu.VMEM((size // split, tokens, 2 * HEAD_DIM), LOW),
         pltpu.VMEM((GROUP,) + pair, LOW), pltpu.VMEM((GROUP,) + pair, LOW),
         pltpu.VMEM(pair, WIDE), pltpu.VMEM(pair, WIDE), pltpu.VMEM((tile, 2 * HEAD_DIM), WIDE),
         pltpu.VMEM((length, HEAD_COLS), LOW), pltpu.VMEM((HEAD_COLS, length), LOW),
-        pltpu.VMEM((4 * size, out_grads.shape[1], HEAD_COLS), LOW),
+        pltpu.VMEM(out_shape[:2] + (HEAD_COLS,), LOW),
         pltpu.VMEM(small.shape, WIDE),
         pltpu.VMEM((3, tokens, width), LOW), pltpu.VMEM((2, size // 2, tokens, width), LOW),
+        pltpu.VMEM(out_shape, LOW),
         dma((2, size // 2)), dma((2, size // 2)), dma((size // split,)), dma((size // split,)), dma,
     ]
     for block in blocks:
@@ -1200,7 +1221,7 @@
         out_shape=[jax.ShapeDtypeStruct((tokens, width), WIDE)]
         + [jax.ShapeDtypeStruct((size,) + block, LOW) for block in blocks]
         + [jax.ShapeDtypeStruct((small_rows, width // 4), WIDE)],
-        in_specs=[vmem, anywhere, anywhere, anywhere] + [vmem] * 14,
+        in_specs=[vmem, anywhere, anywhere] + [vmem] * 16,
         out_specs=[vmem] * 6,
         scratch_shapes=scratch,
         compiler_params=pltpu.CompilerParams(
@@ -1314,9 +1335,7 @@
         normed_two_grad - normed_two * jnp.mean(normed_two_grad * normed_two, axis=-1, keepdims=True)
     )
     project_grad = middle_grad.astype(LOW)
-    out_grad_part = dot("tj,td->jd", mixed_low, project_grad)
     mixed_grad = dot("td,jd->tj", project_grad, out_full).astype(LOW)
-    mixed_grad = mixed_grad.reshape(tokens, KV_HEADS, GROUP * HEAD_DIM).transpose(1, 0, 2)
 
     small_grads = jnp.concatenate(
         [router_part, gain_two_part[None], jnp.zeros((31 - experts, width), WIDE)], axis=0
@@ -1331,23 +1350,25 @@
             mixed_grad,
             gu_grads,
             down_grads,
-            out_grad_part.astype(LOW).reshape(owners, rows, width),
+            mixed_low, project_grad,
             small_grads,
             query_pair, key_value, out_pair, log_total, docs_row, docs_col, places_row,
             cosine, sine, small_full, inputs_all.reshape(length, width), row_scale, head_full,
         ],
         nctx, head_split, 7,
     )
-    gu_home, down_home = gu_home.astype(WIDE), down_home.astype(WIDE)
     out_home, head_home = out_home.astype(WIDE), head_home.astype(WIDE)
     if ff_split == 1:
-        gate_up_gradient = gu_home.reshape(experts, rows, ff2).transpose(1, 0, 2)
-        down_gradient = down_home.reshape(experts, down_rows, width).transpose(1, 0, 2)
+        gate_up_gradient = lax.optimization_barrier(gu_home.reshape(experts, rows, ff2).transpose(1, 0, 2)).astype(WIDE)
+        down_gradient = lax.optimization_barrier(
+            down_home.reshape(experts, down_rows, width).transpose(1, 0, 2)
+        ).astype(WIDE)
     else:
         gate_up_gradient = (
-            gu_home.reshape(experts, ff_split, rows, 2, ff_part).transpose(2, 0, 3, 1, 4).reshape(rows, experts, ff2)
+            gu_home.astype(WIDE).reshape(experts, ff_split, rows, 2, ff_part).transpose(2, 0, 3, 1, 4)
+            .reshape(rows, experts, ff2)
         )
-        down_gradient = down_home.reshape(experts, ff_split, down_rows, width).sum(axis=1).transpose(1, 0, 2)
+        down_gradient = down_home.astype(WIDE).reshape(experts, ff_split, down_rows, width).sum(axis=1).transpose(1, 0, 2)
     output_gradient = out_home.sum(axis=0)
     head_home = head_home.reshape(KV_HEADS, head_split, rows, HEAD_COLS).sum(axis=1).transpose(1, 0, 2)
     query_gradient = head_home[..., : GROUP * HEAD_DIM].reshape(rows, HEADS * HEAD_DIM)

time: 333 us -> 329 us (0.988)
    transpose x2 -> x0, local copies, waits for them, and re-layouts: 4.12 us -> none  [the longest x1 2.54 us: on_device(): gate_up_gradient = gu_home.reshape(experts, rows, ff2).transpose(1, 0, 2)]
    dot_general x6 -> x5, matrix products: 7.91 us -> 6.52 us  [dot(): return jnp.einsum(equation, left, right, preferred_element_type=WIDE)]
where the time goes in v2:
time: 329 us
  Pallas kernels  296 us (90%)
  local copies, waits for them, and re-layouts  12.7 us (4%)
  other arithmetic  12.3 us (4%)
  matrix products  6.52 us (2%)
    pallas_call x1, Pallas kernels, run_front(): pl.pallas_call(functools.partial(front_kernel, size, split, tile), out_sh...  115 us
    pallas_call x1, Pallas kernels, attention_back(): pl.pallas_call(functools.partial(back_kernel, size, split, tile), out_sha...  104 us
    pallas_call x1, Pallas kernels, run_experts(): pl.pallas_call(functools.partial(expert_kernel, size, split), out_shape=[...  76.3 us

profile of v2, /device:TPU:0, one launch (start us, length us, event | category | flops | bytes accessed | tf_op | source)
XLA Modules:
  0.0 328.9 jit_solution(17587223498049832336)
XLA Ops:
  1.3 1.2 multiply_sine_fusion
  2.6 1.8 convert_bitcast_fusion
  4.4 0.0 copy-start.13
  4.4 0.0 copy-start.14
  4.4 1.5 copy.54
  6.0 0.0 copy-done.6
  6.0 0.0 copy-start.12
  6.0 0.0 copy-start.17
  6.0 0.1 convert_bitcast_fusion.1
  6.1 1.1 copy.55
  7.2 0.1 reshape.147
  7.3 0.0 copy-start.1
  7.3 0.1 reshape.148
  7.5 0.1 maximum_bitcast_fusion
  7.6 0.0 copy-done.15
  7.6 0.1 copy.51
  7.7 0.1 copy.52
  7.8 0.0 copy-done.19
  7.8 0.1 copy.53
  7.9 0.1 pad.8.clone
  8.0 0.1 maximum_maximum_fusion
  8.1 0.7 pad_maximum_fusion.pack
  8.8 0.0 copy-done.12
  8.8 0.6 convert_element_type.69.out_rows
  9.5 0.6 broadcast_in_dim.51.docs_in
  10.1 115.1 %run_front.1 = (bf16[8,128,1024]{2,1,0:T(8,128)(2,1)}, bf16[8,128,1024]{2,1,0:T(8,128)(2,1)}, bf16[128,1024]{1,0:T(8,128)(2,1)}, bf16[1024,128]{1,0:T(8,128)(2,1...) custom-call(bf16[128,1024]{1,0:T(8,128)(2,1)} %bitcast.95, ...), custom_call_target="tpu_custom_call" | custom-call | tf_op jit(solution)/shard_map/run_front/pallas_call | solution.py:806
  125.1 0.0 copy-start.7
  125.1 0.0 copy-done.1
  125.1 0.0 copy-start.16
  125.1 2.2 multiply_reduce_fusion.2
  127.4 0.1 fusion.7
  127.6 0.1 multiply_convert_fusion.expert_input
  127.7 0.0 copy-start.2
  127.7 0.7 copy-done.2
  128.4 0.2 fusion.18
  128.6 0.6 fusion.15.combine_rows
  129.2 76.3 %run_experts.1 = (f32[128,1024]{1,0:T(8,128)}, f32[128,1024]{1,0:T(8,128)}, f32[8,8,128]{2,1,0:T(8,128)}, bf16[2,32,32,1024]{3,2,1,0:T(8,128)(2,1)}, bf16[2,32,16,1024]{3,2,1,0:T(8,128)(2,1)}) custom-call(bf16[128,1024]{1,0:T(8,128)(2,1)} %copy-done.2, f32[16,128]{1,0:T(8,128)} %fusion.15.combine_rows, bf16[8,128,1024]{2,1,0:T(8,128)(2,1)} %get-tuple-element.43.upstream, ...), custom_call_target="tpu_custom_call" | custom-call | tf_op jit(solution)/shard_map/run_experts/pallas_call | solution.py:455
  205.6 0.0 copy-start.4
  205.6 0.9 slice.33
  206.6 1.1 fusion.22
  207.7 1.4 multiply_reduce_fusion
  209.1 0.1 pad.2.clone
  209.2 0.7 maximum_bitcast_fusion.1.small
  209.9 0.0 copy-done.4
  209.9 0.2 fusion.19.project_grad
  210.1 0.0 copy-start.3
  210.1 1.6 convolution_convert_fusion.mixed_grad
  211.7 104.4 %attention_back.1 = (f32[128,1024]{1,0:T(8,128)}, bf16[8,2,32,1024]{3,2,1,0:T(8,128)(2,1)}, bf16[8,2,16,1024]{3,2,1,0:T(8,128)(2,1)}, bf16[8,32,1024]{2,1,0:T(8,...) custom-call(bf16[128,1024]{1,0:T(8,128)(2,1)} %convolution_convert_fusion.mixed_grad, ...), custom_call_target="tpu_custom_call" | custom-call | tf_op jit(solution)/shard_map/attention_back/pallas_call | solution.py:1219
  316.1 1.8 copy.70
  317.9 1.6 convert_element_type.78
  319.5 0.3 copy.71
  319.8 1.1 convert_element_type.79
  320.9 0.1 fusion.20
  321.0 0.1 copy.58
  321.1 0.7 reshape.155
  321.8 0.1 copy.59
  321.9 0.7 reshape.156
  322.6 0.0 copy-done.5
  322.6 0.2 fusion.2
  322.8 2.1 fusion.9
  324.9 0.7 copy_bitcast_fusion.2
  325.6 0.7 convert_reduce_fusion
  326.3 1.4 dynamic-slice_bitcast_fusion
  327.7 1.3 dynamic-slice_bitcast_fusion.1
  (45 shorter events, 0.3 us)
Async XLA Ops:
  2.6 3.4 %copy-start.6 = (f32[16,16,1024]{2,1,0:T(8,128)S(1)}, f32[16,16,1024]{2,1,0:T(8,128)}, u32[]{:S(2)}) copy-start(f32[16,16,1024]{2,1,0:T(8,128)} %param.26) | copy-start | bytes 3145732
  4.4 2.8 copy-start.13
  4.4 2.9 copy-start.14
  6.0 1.5 copy-start.11
  6.0 1.6 copy-start.15
  6.0 1.7 copy-start.18
  6.0 1.8 copy-start.19
  6.0 2.8 copy-start.12
  6.0 3.5 %copy-start.17 = (s32[1,128]{1,0:T(1,128)S(1)}, s32[1,128]{1,0:T(1,128)}, u32[]{:S(2)}) copy-start(s32[1,128]{1,0:T(1,128)} %param.15) | copy-start | bytes 1540
  7.3 117.8 %copy-start.1 = (bf16[1,128,1024]{2,1,0:T(8,128)(2,1)S(1)}, bf16[1,128,1024]{2,1,0:T(8,128)(2,1)}, u32[]{:S(2)}) copy-start(bf16[1,128,1024]{2,1,0:T(8,128)(2,1)} %param.14) | copy-start | bytes 786436
  125.1 2.4 copy-start.7
  125.1 2.6 copy-start.16
  127.7 0.7 copy-start.2
  205.6 4.3 %copy-start.4 = (bf16[1,128,1024]{2,1,0:T(8,128)(2,1)S(1)}, bf16[1,128,1024]{2,1,0:T(8,128)(2,1)}, u32[]{:S(2)}) copy-start(bf16[1,128,1024]{2,1,0:T(8,128)(2,1)} %param.27) | copy-start | bytes 786436
  205.6 4.5 %copy-start = (bf16[32,32,1024]{2,1,0:T(8,128)(2,1)S(1)}, bf16[32,32,1024]{2,1,0:T(8,128)(2,1)}, u32[]{:S(2)}) copy-start(bf16[32,32,1024]{2,1,0:T(8,128)(2,1)} %get-tuple-element.41) | copy-start | bytes 6291460
  210.1 1.6 copy-start.3
  317.9 1.6 copy-start.9
  319.5 1.4 copy-start.10
  319.5 3.1 copy-start.5
  322.6 3.0 copy-start.8

commit v3 on v2

--- a/solution.py
+++ b/solution.py
@@ -758,7 +758,7 @@
         out_pair[rows] = result
         blocks = tile // tokens
         head_out[pl.ds(i * blocks, blocks)] = result.astype(LOW).reshape(blocks, tokens, 2 * HEAD_DIM)
-        pump(4)
+        pump(7)
 
     def seat(index):
         return mixed.at[:, pl.ds(pl.multiple_of(index * 2 * HEAD_DIM, 2 * HEAD_DIM), 2 * HEAD_DIM)]

time: 329 us -> 329 us (level)
  no operation moved by 1% of the time
where the time goes in v3:
time: 329 us
  Pallas kernels  296 us (90%)
  local copies, waits for them, and re-layouts  12.7 us (4%)
  other arithmetic  12.3 us (4%)
  matrix products  6.52 us (2%)
    pallas_call x1, Pallas kernels, run_front(): pl.pallas_call(functools.partial(front_kernel, size, split, tile), out_sh...  116 us
    pallas_call x1, Pallas kernels, attention_back(): pl.pallas_call(functools.partial(back_kernel, size, split, tile), out_sha...  103 us
    pallas_call x1, Pallas kernels, run_experts(): pl.pallas_call(functools.partial(expert_kernel, size, split), out_shape=[...  76.7 us

profile of v3, /device:TPU:0, one launch (start us, length us, event | category | flops | bytes accessed | tf_op | source)
XLA Modules:
  0.0 328.9 jit_solution(340967815002682295)
XLA Ops:
  1.3 1.2 multiply_sine_fusion
  2.6 1.8 convert_bitcast_fusion
  4.4 0.0 copy-start.13
  4.4 0.0 copy-start.14
  4.4 1.5 copy.54
  6.0 0.0 copy-start.12
  6.0 0.0 copy-start.17
  6.0 0.1 convert_bitcast_fusion.1
  6.1 1.1 copy.55
  7.2 0.0 copy-done.13
  7.2 0.1 reshape.147
  7.3 0.0 copy-start.1
  7.3 0.1 reshape.148
  7.5 0.1 maximum_bitcast_fusion
  7.6 0.0 copy-done.15
  7.6 0.1 copy.51
  7.7 0.1 copy.52
  7.8 0.0 copy-done.19
  7.8 0.1 copy.53
  7.9 0.1 pad.8.clone
  8.0 0.1 maximum_maximum_fusion
  8.1 0.7 pad_maximum_fusion.pack
  8.8 0.0 copy-done.12
  8.8 0.6 convert_element_type.69.out_rows
  9.5 0.6 broadcast_in_dim.51.docs_in
  10.1 115.7 %run_front.1 = (bf16[8,128,1024]{2,1,0:T(8,128)(2,1)}, bf16[8,128,1024]{2,1,0:T(8,128)(2,1)}, bf16[128,1024]{1,0:T(8,128)(2,1)}, bf16[1024,128]{1,0:T(8,128)(2,1...) custom-call(bf16[128,1024]{1,0:T(8,128)(2,1)} %bitcast.95, ...), custom_call_target="tpu_custom_call" | custom-call | tf_op jit(solution)/shard_map/run_front/pallas_call | solution.py:806
  125.7 0.0 copy-start.16
  125.8 2.3 multiply_reduce_fusion.2
  128.0 0.1 fusion.7
  128.2 0.1 multiply_convert_fusion.expert_input
  128.3 0.0 copy-start.2
  128.3 0.0 copy-done.16
  128.3 0.7 copy-done.2
  129.0 0.2 fusion.18
  129.2 0.6 fusion.15.combine_rows
  129.9 76.7 %run_experts.1 = (f32[128,1024]{1,0:T(8,128)}, f32[128,1024]{1,0:T(8,128)}, f32[8,8,128]{2,1,0:T(8,128)}, bf16[2,32,32,1024]{3,2,1,0:T(8,128)(2,1)}, bf16[2,32,16,1024]{3,2,1,0:T(8,128)(2,1)}) custom-call(bf16[128,1024]{1,0:T(8,128)(2,1)} %copy-done.2, f32[16,128]{1,0:T(8,128)} %fusion.15.combine_rows, bf16[8,128,1024]{2,1,0:T(8,128)(2,1)} %get-tuple-element.43.upstream, ...), custom_call_target="tpu_custom_call" | custom-call | tf_op jit(solution)/shard_map/run_experts/pallas_call | solution.py:455
  206.5 0.0 copy-start.4
  206.5 0.9 slice.33
  207.5 1.1 fusion.22
  208.6 1.4 multiply_reduce_fusion
  210.0 0.1 pad.2.clone
  210.1 0.7 maximum_bitcast_fusion.1.small
  210.9 0.0 copy-done.4
  210.9 0.2 fusion.19.project_grad
  211.1 0.0 copy-start.3
  211.1 1.6 convolution_convert_fusion.mixed_grad
  212.7 103.4 %attention_back.1 = (f32[128,1024]{1,0:T(8,128)}, bf16[8,2,32,1024]{3,2,1,0:T(8,128)(2,1)}, bf16[8,2,16,1024]{3,2,1,0:T(8,128)(2,1)}, bf16[8,32,1024]{2,1,0:T(8,...) custom-call(bf16[128,1024]{1,0:T(8,128)(2,1)} %convolution_convert_fusion.mixed_grad, ...), custom_call_target="tpu_custom_call" | custom-call | tf_op jit(solution)/shard_map/attention_back/pallas_call | solution.py:1219
  316.1 1.8 copy.70
  317.9 1.6 convert_element_type.78
  319.5 0.3 copy.71
  319.8 1.1 convert_element_type.79
  320.9 0.0 copy-done.10
  320.9 0.1 fusion.20
  321.0 0.1 copy.58
  321.1 0.7 reshape.155
  321.8 0.1 copy.59
  321.9 0.7 reshape.156
  322.6 0.2 fusion.2
  322.8 2.1 fusion.9
  324.9 0.7 copy_bitcast_fusion.2
  325.6 0.0 copy-done.8
  325.6 0.7 convert_reduce_fusion
  326.3 1.4 dynamic-slice_bitcast_fusion
  327.7 1.3 dynamic-slice_bitcast_fusion.1
  (45 shorter events, 0.3 us)
Async XLA Ops:
  2.6 3.4 %copy-start.6 = (f32[16,16,1024]{2,1,0:T(8,128)S(1)}, f32[16,16,1024]{2,1,0:T(8,128)}, u32[]{:S(2)}) copy-start(f32[16,16,1024]{2,1,0:T(8,128)} %param.26) | copy-start | bytes 3145732
  4.4 2.8 copy-start.13
  4.4 2.9 copy-start.14
  6.0 1.5 copy-start.11
  6.0 1.6 copy-start.15
  6.0 1.7 copy-start.18
  6.0 1.8 copy-start.19
  6.0 2.8 copy-start.12
  6.0 3.5 %copy-start.17 = (s32[1,128]{1,0:T(1,128)S(1)}, s32[1,128]{1,0:T(1,128)}, u32[]{:S(2)}) copy-start(s32[1,128]{1,0:T(1,128)} %param.15) | copy-start | bytes 1540
  7.3 118.4 %copy-start.1 = (bf16[1,128,1024]{2,1,0:T(8,128)(2,1)S(1)}, bf16[1,128,1024]{2,1,0:T(8,128)(2,1)}, u32[]{:S(2)}) copy-start(bf16[1,128,1024]{2,1,0:T(8,128)(2,1)} %param.14) | copy-start | bytes 786436
  125.7 2.4 copy-start.7
  125.7 2.6 copy-start.16
  128.3 0.7 copy-start.2
  206.5 4.3 %copy-start.4 = (bf16[1,128,1024]{2,1,0:T(8,128)(2,1)S(1)}, bf16[1,128,1024]{2,1,0:T(8,128)(2,1)}, u32[]{:S(2)}) copy-start(bf16[1,128,1024]{2,1,0:T(8,128)(2,1)} %param.27) | copy-start | bytes 786436
  206.5 4.5 %copy-start = (bf16[32,32,1024]{2,1,0:T(8,128)(2,1)S(1)}, bf16[32,32,1024]{2,1,0:T(8,128)(2,1)}, u32[]{:S(2)}) copy-start(bf16[32,32,1024]{2,1,0:T(8,128)(2,1)} %get-tuple-element.41) | copy-start | bytes 6291460
  211.1 1.6 copy-start.3
  317.9 1.6 copy-start.9
  319.5 1.4 copy-start.10
  319.5 3.1 copy-start.5
  322.6 3.0 copy-start.8
